TPU v7x, 256 devices: a whole 4x4x8 slice. The times are simulated.
256 devices in a mesh: dp: 16 (over z_hi, y, core), bulk: 16 (over x, z_lo).
Axes of the slice: x: 4, y: 4, z: 8 (z_hi: 2, z_lo: 4; z = z_hi * 4 + z_lo), core: 2. Of those that a mesh axis runs over, the one named last changes fastest.
Arguments:
- node_feats: bfloat16 [196608, 512], P(('dp', 'bulk')), may hold values from -6 to 6
- edge_feats: bfloat16 [262144, 512], P(('dp', 'bulk')), may hold values from -6 to 6
- grad_nodes: bfloat16 [196608, 512], P(('dp', 'bulk')), may hold values from -6 to 6
- grad_edges: bfloat16 [262144, 512], P(('dp', 'bulk')), may hold values from -6 to 6
- sources: int32 [262144], P(('dp', 'bulk')), may hold values from 0 to 1023
- tile_blocks: int32 [2048], P(('dp', 'bulk')), may hold values from 0 to 5
- offsets: int32 [262144], P(('dp', 'bulk')), may hold values from 0 to 127
- edge_count: int32 [256], P(('dp', 'bulk')), may hold values from 512 to 1024, as said below
- weights: bfloat16 [3584, 512], replicated
Outputs:
- node_grads: bfloat16 [196608, 512], P(('dp', 'bulk'))
- edge_grads: bfloat16 [262144, 512], P(('dp', 'bulk'))
- weight_grads: float32 [3584, 512], P('dp')
Inputs may be any that keep to these rules, and one draw needn't show every extreme that they name: `sources`: rows 0 to 127 and the last 128 rows of a slab's extended list are the neighbours' boundary nodes. `edge_count`: some slab is full in every draw.
All inputs are finite; a program needn't handle non-finite values.
Results may differ from a plain program's by a relative error of at most 0.0065.
Values may be sent and summed in bfloat16 or wider, within the bound.
A program may use at most 128 MiB of HBM per device.

v0:
```python
import jax
import jax.numpy as jnp
from jax import lax
from jax.sharding import PartitionSpec as P

HALO = 128


def extended_2(block, sides, width):
    for axis, dim in sides:
        count = lax.axis_size(axis)
        forward = [(i, i + 1) for i in range(count - 1)]
        backward = [(target, source) for source, target in forward]
        low = lax.ppermute(
            lax.slice_in_dim(block, block.shape[dim] - width, None, axis=dim), axis, forward
        )
        high = lax.ppermute(lax.slice_in_dim(block, 0, width, axis=dim), axis, backward)
        block = jnp.concatenate([low, block, high], axis=dim)
    return block


def shifted(value, axis, steps):
    count = lax.axis_size(axis)
    initial, last = (max(0, -steps), min(count, count - steps))
    return lax.ppermute(value, axis, [(source, source + steps) for source in range(initial, last)])


def ln_core(values):
    middle = values - jnp.mean(values, -1, keepdims=True)
    spread = jnp.mean(middle * middle, -1, keepdims=True)
    return middle * lax.rsqrt(spread + 1e-05)


def ln_back(values, cotangent):
    unused, pull = jax.vjp(ln_core, values)
    return pull(cotangent)[0]


def silu_back(values, cotangent):
    sigma = jax.nn.sigmoid(values)
    return cotangent * sigma * (1.0 + values * (1.0 - sigma))


def left_dot(first, second):
    return lax.dot_general(
        first, second, (((0,), (0,)), ((), ())), preferred_element_type=jnp.float32
    )


def right_dot(first, second):
    return lax.dot_general(
        first, second, (((1,), (1,)), ((), ())), preferred_element_type=jnp.float32
    )


def slab_backward(
    extended, edge_feats, grad_nodes, grad_edges, sources, tile_blocks, offsets, count, weights
):
    width = weights.shape[1]
    own_rows = grad_nodes.shape[0]
    rim = (extended.shape[0] - own_rows) // 2
    ntiles = tile_blocks.shape[0]
    nedges = offsets.shape[0]
    tile = nedges // ntiles
    nblocks = own_rows // tile
    w_edge_one = weights[: 3 * width]
    w_edge_two = weights[3 * width : 4 * width]
    w_node_one = weights[4 * width : 6 * width]
    w_node_two = weights[6 * width :]
    dest = jnp.repeat(tile_blocks, tile) * tile + offsets
    live = (jnp.arange(nedges) < count).astype(jnp.float32)[:, None]
    joined = jnp.concatenate([extended[sources], extended[dest + rim], edge_feats], 1)
    act_one = jnp.dot(joined, w_edge_one, preferred_element_type=jnp.float32)
    hidden_one = jax.nn.silu(act_one).astype(jnp.bfloat16)
    act_two = jnp.dot(hidden_one, w_edge_two, preferred_element_type=jnp.float32)
    message = (ln_core(act_two) * live).astype(jnp.bfloat16)
    onehot = (offsets.reshape(ntiles, tile)[:, :, None] == jnp.arange(tile)[None, None, :]).astype(
        jnp.bfloat16
    )
    pertile = jnp.einsum(
        "tek,teh->tkh",
        onehot,
        message.reshape(ntiles, tile, width),
        preferred_element_type=jnp.float32,
    )
    gathered = jnp.zeros((nblocks, tile, width), jnp.float32).at[tile_blocks].add(pertile)
    aggregate = gathered.reshape(own_rows, width).astype(jnp.bfloat16)
    own_feats = extended[rim : rim + own_rows]
    joined_nodes = jnp.concatenate([own_feats, aggregate], 1)
    node_one = jnp.dot(joined_nodes, w_node_one, preferred_element_type=jnp.float32)
    node_hidden = jax.nn.silu(node_one).astype(jnp.bfloat16)
    node_two = jnp.dot(node_hidden, w_node_two, preferred_element_type=jnp.float32)
    d_node_two = ln_back(node_two, grad_nodes.astype(jnp.float32)).astype(jnp.bfloat16)
    g_node_two = left_dot(node_hidden, d_node_two)
    d_node_one = silu_back(node_one, right_dot(d_node_two, w_node_two)).astype(jnp.bfloat16)
    g_node_one = left_dot(joined_nodes, d_node_one)
    d_inputs = right_dot(d_node_one, w_node_one)
    d_aggregate = d_inputs[:, width:].astype(jnp.bfloat16)
    pulled = d_aggregate.reshape(nblocks, tile, width)[tile_blocks]
    d_message = jnp.einsum(
        "tek,tkh->teh", onehot, pulled, preferred_element_type=jnp.float32
    ).reshape(nedges, width)
    d_msg_total = live * (d_message + grad_edges.astype(jnp.float32))
    d_act_two = ln_back(act_two, d_msg_total).astype(jnp.bfloat16)
    g_edge_two = left_dot(hidden_one, d_act_two)
    d_act_one = silu_back(act_one, right_dot(d_act_two, w_edge_two)).astype(jnp.bfloat16)
    g_edge_one = left_dot(joined, d_act_one)
    d_joined = right_dot(d_act_one, w_edge_one)
    edge_grads = (grad_edges.astype(jnp.float32) + d_joined[:, 2 * width :]).astype(jnp.bfloat16)
    d_extended = jnp.zeros((extended.shape[0], width), jnp.float32)
    d_extended = d_extended.at[sources].add(d_joined[:, :width])
    d_extended = d_extended.at[dest + rim].add(d_joined[:, width : 2 * width])
    d_extended = d_extended.at[rim : rim + own_rows].add(
        grad_nodes.astype(jnp.float32) + d_inputs[:, :width]
    )
    grads = jnp.concatenate([g_edge_one, g_edge_two, g_node_one, g_node_two], 0)
    return (d_extended, edge_grads, grads)


def body(
    node_feats,
    edge_feats,
    grad_nodes,
    grad_edges,
    sources,
    tile_blocks,
    offsets,
    edge_count,
    weights,
):
    extended = extended_2(node_feats, (("bulk", 0),), HALO)
    d_extended, edge_grads, grads = slab_backward(
        extended,
        edge_feats,
        grad_nodes,
        grad_edges,
        sources,
        tile_blocks,
        offsets,
        edge_count[0],
        weights,
    )
    own_rows = node_feats.shape[0]
    from_after = shifted(d_extended[:HALO].astype(jnp.bfloat16), "bulk", -1).astype(jnp.float32)
    from_before = shifted(d_extended[HALO + own_rows :].astype(jnp.bfloat16), "bulk", 1).astype(
        jnp.float32
    )
    own = d_extended[HALO : HALO + own_rows]
    own = own.at[:HALO].add(from_before)
    own = own.at[own_rows - HALO :].add(from_after)
    node_grads = own.astype(jnp.bfloat16)
    slab_total = lax.psum(grads, "bulk")
    summed = lax.psum_scatter(slab_total, "dp", scatter_dimension=0, tiled=True)
    factor = 1.0 / jnp.sqrt(
        jnp.float32(lax.axis_size("dp") * lax.axis_size("bulk") * edge_feats.shape[0])
    )
    return (node_grads, edge_grads, summed * factor)


def solution(mesh):
    in_specs = (
        P(("dp", "bulk"), None),
        P(("dp", "bulk"), None),
        P(("dp", "bulk"), None),
        P(("dp", "bulk"), None),
        P(("dp", "bulk")),
        P(("dp", "bulk")),
        P(("dp", "bulk")),
        P(("dp", "bulk")),
        P(),
    )
    out_specs = (P(("dp", "bulk"), None), P(("dp", "bulk"), None), P("dp", None))
    return jax.shard_map(body, mesh=mesh, in_specs=in_specs, out_specs=out_specs, check_vma=False)
```

profile of v0, /device:TPU:8, one launch (start us, length us, event | category | flops | bytes accessed | tf_op | source)
XLA Modules:
  0.0 380.9 jit_solution(7735574067634619615)
XLA Ops:
  7.2 0.0 reduce-scatter.2.cloned.1.call-start
  7.2 1.1 fusion.40
  8.3 1.3 collective-permute-start.1
  9.6 4.6 %collective-permute-start = (bf16[128,512]{1,0:T(8,128)(2,1)S(1)}, bf16[128,512]{1,0:T(8,128)(2,1)S(1)}, u32[]{:S(2)}, u32[]{:S(2)}) collective-permute-start(bf16[128,512]{1,0:T(8,128)(2,1)S(1)} %get-tuple-element.54), channel_id=1, source_target_pairs={{0,1},{1,2},{2,3},{3,4},{4,5},{5,6},{6,7},{7,8},{8,9},{9,10},{10,1... | collective-permute-start | bytes 393224 | tf_op jit(solution)/shard_map/ppermute | solution.py:14
  14.8 0.7 broadcast_multiply_fusion.3
  15.4 0.8 compare_select_fusion.1
  16.2 1.4 copy.18
  17.7 0.1 constant_dynamic-update-slice_fusion.1
  17.8 4.0 %gather_fusion.1 = bf16[1024,512]{1,0:T(8,128)(2,1)S(1)} fusion(bf16[1024,512]{1,0:T(8,128)(2,1)S(1)} %constant_dynamic-update-slice_fusion, s32[1024]{0:T(1024)S(1)} %get-tuple-element.67), kind=kCustom, calls=%fused_computation.1 | custom fusion | bytes 2101248 | tf_op jit(solution)/shard_map/gather | solution.py:72
  21.8 5.1 %gather_fusion = bf16[1024,512]{1,0:T(8,128)(2,1)} fusion(bf16[1024,512]{1,0:T(8,128)(2,1)S(1)} %constant_dynamic-update-slice_fusion, s32[1024]{0:T(1024)S(1)} %get-tuple-element.56), kind=kCustom, calls=%fused_computation | custom fusion | bytes 2101248 | tf_op jit(solution)/shard_map/gather | solution.py:72
  26.8 1.4 constant_dynamic-update-slice_fusion.5
  28.2 0.1 constant_dynamic-update-slice_fusion.4
  28.3 0.1 copy-done.9
  28.4 0.1 constant_dynamic-update-slice_fusion.3
  28.5 1.9 copy-done.12
  30.3 3.3 multiply_convert_fusion.2
  33.7 0.8 fusion.41
  34.5 0.4 multiply_reduce_fusion.1
  34.9 0.5 multiply_convert_fusion.1
  35.4 0.2 copy-done.16
  35.6 2.2 fusion.20
  37.8 1.4 broadcast_in_dim.43
  39.2 4.9 %scatter_fusion = f32[6,128,512]{2,1,0:T(8,128)} fusion(f32[6,128,512]{2,1,0:T(8,128)} %broadcast_in_dim.43, s32[8]{0:T(128)S(1)} %get-tuple-element.60, f32[8,128,512]{2,1,0:T(8,128)} %fusion.20), kind=kCustom, calls=%fused_computation.3 | custom fusion | flops 524288 | bytes 6291488 | tf_op jit(solution)/shard_map/scatter-add | solution.py:86
  44.1 1.6 convert_element_type.62
  45.7 0.0 copy-done.7
  45.7 2.3 fusion.14
  48.1 0.7 fusion.42
  48.8 0.3 multiply_reduce_fusion.2
  49.2 0.4 fusion.18
  49.6 0.4 add_convert_fusion.1
  50.0 0.9 multiply_convert_fusion.3
  51.0 1.6 fusion.37
  52.6 2.4 fusion.13
  54.9 1.0 fusion.15
  56.0 1.7 copy-done
  57.7 1.0 slice.161
  58.6 2.7 gather_fusion.2
  61.4 1.8 fusion.19
  63.2 0.8 multiply_reduce_fusion
  64.0 1.6 fusion.38
  65.7 0.8 fusion.36
  66.4 0.8 copy-done.18
  67.2 2.4 multiply_convert_fusion
  69.7 1.0 copy-done.17
  70.6 1.9 fusion.43
  72.5 3.5 pad_maximum_fusion
  76.0 0.0 reduce-scatter.2.cloned.1.call-update
  76.1 0.0 all-reduce.2.cloned.1.call-start
  76.1 1.4 slice-done
  77.5 1.6 copy.25
  79.1 6.2 %fusion.8 = f32[1024,1536]{1,0:T(8,128)} fusion(bf16[1024,512]{1,0:T(8,128)(2,1)} %copy-done.17, bf16[3584,512]{1,0:T(8,128)(2,1)} %param.23), kind=kOutput, calls=%fused_computation.36 | convolution fusion | flops 1610612736 | bytes 8912896 | tf_op jit(solution)/shard_map/dot_general | solution.py:51
  85.3 8.8 %scatter_custom_fusion.1 = f32[1024,512]{1,0:T(8,128)} fusion(s32[1024]{0:T(1024)S(1)} %get-tuple-element.55, f32[1024,1536]{1,0:T(8,128)} %fusion.8, f32[]{:T(128)} %constant.111.clone.1), kind=kCustom, calls=%fused_computation.18 | custom fusion | flops 524288 | bytes 4194816 | tf_op jit(solution)/shard_map/scatter-add | solution.py:111
  94.1 10.4 %scatter_custom_fusion.2 = f32[1024,512]{1,0:T(8,128)} fusion(f32[1024,512]{1,0:T(8,128)} %scatter_custom_fusion.1, s32[1024]{0:T(1024)S(1)} %get-tuple-element.68, f32[1024,1536]{1,0:T(8,128)} %fusion.8), kind=kCustom, calls=%fused_computation.16 | custom fusion | flops 524288 | bytes 4194304 | tf_op jit(solution)/shard_map/scatter-add | solution.py:112
  104.5 2.1 copy.20
  106.6 0.2 convert.8
  106.8 4.2 %collective-permute-start.2 = (bf16[128,512]{0,1:T(8,128)(2,1)S(1)}, bf16[128,512]{0,1:T(8,128)(2,1)S(1)}, u32[]{:S(2)}, u32[]{:S(2)}) collective-permute-start(bf16[128,512]{0,1:T(8,128)(2,1)S(1)} %get-tuple-element.52), channel_id=1, source_target_pairs={{0,1},{1,2},{2,3},{3,4},{4,5},{5,6},{6,7},{7,8},{8,9},{9,10},{10,1... | collective-permute-start | bytes 393224 | tf_op jit(solution)/shard_map/ppermute | solution.py:25
  111.0 1.4 fusion.7
  112.5 3.0 fusion.1
  115.5 1.3 collective-permute-start.3
  116.8 97.5 %reduce-scatter.2.cloned.1.call-done = f32[224,512]{1,0:T(8,128)} async-done(((f32[3584,512]{1,0:T(8,128)}), f32[224,512]{1,0:T(8,128)}) %reduce-scatter.2.cloned.1.call-update) | async-done | bytes 458768 | tf_op jit(solution)/shard_map/reduce_scatter | solution.py:153
  214.4 0.1 convert_element_type.72
  214.5 1.2 copy.23
  215.7 156.6 %all-reduce.2.cloned.1.call-done = f32[224,512]{1,0:T(8,128)} async-done(((f32[224,512]{1,0:T(8,128)}), f32[224,512]{1,0:T(8,128)}) %all-reduce.2.cloned.1.call-update) | async-done | bytes 458768 | tf_op jit(solution)/shard_map/psum | solution.py:152
  372.2 1.8 broadcast_multiply_fusion
  (51 shorter events, 0.3 us)
Async XLA Ops:
  7.2 10.5 %copy-start.6 = (bf16[768,512]{1,0:T(8,128)(2,1)S(1)}, bf16[768,512]{1,0:T(8,128)(2,1)}, u32[]{:S(2)}) copy-start(bf16[768,512]{1,0:T(8,128)(2,1)} %param.15) | copy-start | bytes 2359300
  7.2 207.1 %reduce-scatter.2.cloned.1.call-start = ((), (), s32[]{:S(2)}) async-start(), calls=%async_computation.1 | async-start | bytes 7798784 | tf_op jit(solution)/shard_map/reduce_scatter | solution.py:153
  8.3 9.5 %collective-permute-start.1 = (bf16[128,512]{1,0:T(8,128)(2,1)S(1)}, bf16[128,512]{1,0:T(8,128)(2,1)S(1)}, u32[]{:S(2)}, u32[]{:S(2)}) collective-permute-start(bf16[128,512]{1,0:T(8,128)(2,1)S(1)} %get-tuple-element.53), channel_id=1, source_target_pairs={{1,0},{2,1},{3,2},{4,3},{5,4},{6,5},{7,6},{8,7},{9,8},{10,9},{11,1... | collective-permute-start | bytes 393224 | tf_op jit(solution)/shard_map/ppermute | solution.py:17
  9.6 8.1 %collective-permute-start = (bf16[128,512]{1,0:T(8,128)(2,1)S(1)}, bf16[128,512]{1,0:T(8,128)(2,1)S(1)}, u32[]{:S(2)}, u32[]{:S(2)}) collective-permute-start(bf16[128,512]{1,0:T(8,128)(2,1)S(1)} %get-tuple-element.54), channel_id=1, source_target_pairs={{0,1},{1,2},{2,3},{3,4},{4,5},{5,6},{6,7},{7,8},{8,9},{9,10},{10,1... | collective-permute-start | bytes 393224 | tf_op jit(solution)/shard_map/ppermute | solution.py:14
  26.8 1.5 copy-start.9
  28.2 2.1 copy-start.12
  30.3 3.4 copy-start.14
  33.7 1.2 copy-start.10
  34.9 0.7 copy-start.16
  44.1 1.6 copy-start.7
  45.7 2.4 copy-start.13
  55.9 1.7 copy-start
  61.4 1.8 copy-start.1
  64.0 1.6 copy-start.11
  65.6 1.6 copy-start.18
  67.2 3.4 copy-start.15
  69.6 1.0 copy-start.17
  70.6 1.9 copy-start.5
  70.6 1.9 copy-start.8
  76.0 1.4 slice-start
  76.1 296.2 %all-reduce.2.cloned.1.call-start = ((), (), s32[]{:S(2)}) async-start(), calls=%async_computation.2 | async-start | bytes 917504 | tf_op jit(solution)/shard_map/psum | solution.py:152
  106.6 4.4 %copy-start.4 = (f32[768,512]{0,1:T(8,128)S(1)}, f32[768,512]{0,1:T(8,128)}, u32[]{:S(2)}) copy-start(f32[768,512]{0,1:T(8,128)} %copy.25) | copy-start | bytes 4718596
  106.8 5.7 %copy-start.2 = (bf16[1024,512]{1,0:T(8,128)(2,1)S(1)}, bf16[1024,512]{1,0:T(8,128)(2,1)}, u32[]{:S(2)}) copy-start(bf16[1024,512]{1,0:T(8,128)(2,1)} %param.18) | copy-start | bytes 3145732
  106.8 107.5 %collective-permute-start.2 = (bf16[128,512]{0,1:T(8,128)(2,1)S(1)}, bf16[128,512]{0,1:T(8,128)(2,1)S(1)}, u32[]{:S(2)}, u32[]{:S(2)}) collective-permute-start(bf16[128,512]{0,1:T(8,128)(2,1)S(1)} %get-tuple-element.52), channel_id=1, source_target_pairs={{0,1},{1,2},{2,3},{3,4},{4,5},{5,6},{6,7},{7,8},{8,9},{9,10},{10,1... | collective-permute-start | bytes 393224 | tf_op jit(solution)/shard_map/ppermute | solution.py:25
  112.5 101.8 %copy-start.3 = (f32[768,512]{0,1:T(8,128)S(1)}, f32[768,512]{0,1:T(8,128)}, u32[]{:S(2)}) copy-start(f32[768,512]{0,1:T(8,128)} %fusion.7) | copy-start | bytes 4718596
  115.5 98.9 %collective-permute-start.3 = (bf16[128,512]{0,1:T(8,128)(2,1)S(1)}, bf16[128,512]{0,1:T(8,128)(2,1)S(1)}, u32[]{:S(2)}, u32[]{:S(2)}) collective-permute-start(bf16[128,512]{0,1:T(8,128)(2,1)S(1)} %get-tuple-element.51), channel_id=1, source_target_pairs={{1,0},{2,1},{3,2},{4,3},{5,4},{6,5},{7,6},{8,7},{9,8},{10,9},{11,1... | collective-permute-start | bytes 393224 | tf_op jit(solution)/shard_map/ppermute | solution.py:25
Sparse Core Ops, SparseCore 0:
  76.2 138.0 reduce-scatter.1
  216.9 155.2 all-reduce.1
where the time goes:
time: 382 us; the launch traced here: 381 us
  waiting for transfers between devices  254 us (66%)
  other arithmetic  41.8 us (11%)
  local copies, waits for them, and re-layouts  30.1 us (8%)
  matrix products  28.4 us (7%)
  between operations  15.1 us (4%)
  starting transfers between devices  11.4 us (3%)
    psum x1, waiting for transfers between devices, body(): slab_total = lax.psum(grads, 'bulk')  157 us
    reduce_scatter x1, waiting for transfers between devices, body(): summed = lax.psum_scatter(slab_total, 'dp', scatter_dimension=0, tiled=True)  97.5 us
    unnamed x45, local copies, waits for them, and re-layouts  11.3 us
    dot_general x4, matrix products, right_dot(): lax.dot_general(first, second, (((1,), (1,)), ((), ())), preferred_elemen...  10.6 us
    scatter-add x1, other arithmetic, slab_backward(): d_extended = d_extended.at[dest + rim].add(d_joined[:, width:2 * width])  10.4 us
    scatter-add x1, other arithmetic, slab_backward(): d_extended = d_extended.at[sources].add(d_joined[:, :width])  8.78 us
  transfers between devices with their start and end apart: 6, of which 2 were waited for; matrix products, arithmetic and copies ran while one was open for 10% of the time, Pallas kernels for 0%

commit v1 on v0

--- a/solution.py
+++ b/solution.py
@@ -1,6 +1,8 @@
 import jax
 import jax.numpy as jnp
+import numpy as np
 from jax import lax
+from jax.sharding import Mesh
 from jax.sharding import PartitionSpec as P
 
 HALO = 128
@@ -8,7 +10,7 @@
 
 def extended_2(block, sides, width):
     for axis, dim in sides:
-        count = lax.axis_size(axis)
+        count = axis_count(axis)
         forward = [(i, i + 1) for i in range(count - 1)]
         backward = [(target, source) for source, target in forward]
         low = lax.ppermute(
@@ -19,8 +21,12 @@
     return block
 
 
+def axis_count(axis):
+    return int(np.prod([lax.axis_size(name) for name in axis]))
+
+
 def shifted(value, axis, steps):
-    count = lax.axis_size(axis)
+    count = axis_count(axis)
     initial, last = (max(0, -steps), min(count, count - steps))
     return lax.ppermute(value, axis, [(source, source + steps) for source in range(initial, last)])
 
@@ -117,6 +123,24 @@
     return (d_extended, edge_grads, grads)
 
 
+DP = ("zh", "y", "c")
+BULK = ("x", "zl")
+
+
+def reduce_grads(grads):
+    sizes = [lax.axis_size(name) for name in DP]
+    rows = grads.shape[0] // int(np.prod(sizes))
+    order = ("c", "y", "zh")
+    blocks = grads.reshape(*sizes, rows, grads.shape[1])
+    blocks = blocks.transpose([DP.index(name) for name in order] + [3, 4])
+    part = blocks.reshape(grads.shape)
+    for name in order + ("zl", "x"):
+        part = lax.psum_scatter(part, name, scatter_dimension=0, tiled=True)
+    for name in ("x", "zl"):
+        part = lax.all_gather(part, name, axis=0, tiled=True)
+    return part
+
+
 def body(
     node_feats,
     edge_feats,
@@ -128,7 +152,7 @@
     edge_count,
     weights,
 ):
-    extended = extended_2(node_feats, (("bulk", 0),), HALO)
+    extended = extended_2(node_feats, ((BULK, 0),), HALO)
     d_extended, edge_grads, grads = slab_backward(
         extended,
         edge_feats,
@@ -141,33 +165,25 @@
         weights,
     )
     own_rows = node_feats.shape[0]
-    from_after = shifted(d_extended[:HALO].astype(jnp.bfloat16), "bulk", -1).astype(jnp.float32)
-    from_before = shifted(d_extended[HALO + own_rows :].astype(jnp.bfloat16), "bulk", 1).astype(
+    from_after = shifted(d_extended[:HALO].astype(jnp.bfloat16), BULK, -1).astype(jnp.float32)
+    from_before = shifted(d_extended[HALO + own_rows :].astype(jnp.bfloat16), BULK, 1).astype(
         jnp.float32
     )
     own = d_extended[HALO : HALO + own_rows]
     own = own.at[:HALO].add(from_before)
     own = own.at[own_rows - HALO :].add(from_after)
     node_grads = own.astype(jnp.bfloat16)
-    slab_total = lax.psum(grads, "bulk")
-    summed = lax.psum_scatter(slab_total, "dp", scatter_dimension=0, tiled=True)
-    factor = 1.0 / jnp.sqrt(
-        jnp.float32(lax.axis_size("dp") * lax.axis_size("bulk") * edge_feats.shape[0])
-    )
+    summed = reduce_grads(grads)
+    factor = 1.0 / jnp.sqrt(jnp.float32(axis_count(DP + BULK) * edge_feats.shape[0]))
     return (node_grads, edge_grads, summed * factor)
 
 
 def solution(mesh):
-    in_specs = (
-        P(("dp", "bulk"), None),
-        P(("dp", "bulk"), None),
-        P(("dp", "bulk"), None),
-        P(("dp", "bulk"), None),
-        P(("dp", "bulk")),
-        P(("dp", "bulk")),
-        P(("dp", "bulk")),
-        P(("dp", "bulk")),
-        P(),
-    )
-    out_specs = (P(("dp", "bulk"), None), P(("dp", "bulk"), None), P("dp", None))
-    return jax.shard_map(body, mesh=mesh, in_specs=in_specs, out_specs=out_specs, check_vma=False)
+    devices = np.asarray(mesh.devices)
+    shape = (2, devices.shape[0] // 4, 2, devices.shape[1] // 4, 4)
+    fine = Mesh(devices.reshape(shape), DP + BULK)
+    rows = P(DP + BULK, None)
+    flat = P(DP + BULK)
+    in_specs = (rows, rows, rows, rows, flat, flat, flat, flat, P())
+    out_specs = (rows, rows, P(DP, None))
+    return jax.shard_map(body, mesh=fine, in_specs=in_specs, out_specs=out_specs, check_vma=False)

time: 382 us -> 278 us (0.73)
  waiting for transfers between devices: 254 us -> 102 us
  blocking collectives: 0 us -> 39.1 us
    psum x1 -> x0, waiting for transfers between devices: 157 us -> none  [body(): slab_total = lax.psum(grads, 'bulk')]
    all_gather x0 -> x2, blocking collectives: none -> 26.6 us  [reduce_grads(): part = lax.all_gather(part, name, axis=0, tiled=True)]
    unnamed x0 -> x1, blocking collectives: none -> 12.6 us
    reduce_scatter x1 -> x4, waiting for transfers between devices: 97.5 us -> 102 us  [reduce_grads(): part = lax.psum_scatter(part, name, scatter_dimension=0, tiled=True)]
    reshape x0 -> x1, local copies, waits for them, and re-layouts: none -> 4.13 us  [reduce_grads(): blocks = grads.reshape(*sizes, rows, grads.shape[1])]
    unnamed x45 -> x48, local copies, waits for them, and re-layouts: 11.3 us -> 12.2 us
  transfers between devices with their start and end apart: 6 -> 9, of which waited for: 2 -> 4; matrix products, arithmetic and copies ran while one was open for 10% -> 21% of each run, Pallas kernels for 0% -> 0%
where the time goes in v1:
time: 278 us; the launch traced here: 277 us
  waiting for transfers between devices  102 us (37%)
  other arithmetic  44.1 us (16%)
  blocking collectives  39.1 us (14%)
  local copies, waits for them, and re-layouts  33.7 us (12%)
  matrix products  28.4 us (10%)
  between operations  15.6 us (6%)
  starting transfers between devices  13.9 us (5%)
    reduce_scatter x4, waiting for transfers between devices, reduce_grads(): part = lax.psum_scatter(part, name, scatter_dimension=0, tiled=True)  102 us
    all_gather x2, blocking collectives, reduce_grads(): part = lax.all_gather(part, name, axis=0, tiled=True)  26.6 us
    unnamed x1, blocking collectives  12.6 us
    unnamed x48, local copies, waits for them, and re-layouts  12.2 us
    dot_general x4, matrix products, right_dot(): lax.dot_general(first, second, (((1,), (1,)), ((), ())), preferred_elemen...  10.6 us
    scatter-add x1, other arithmetic, slab_backward(): d_extended = d_extended.at[dest + rim].add(d_joined[:, width:2 * width])  10.3 us
    scatter-add x1, other arithmetic, slab_backward(): d_extended = d_extended.at[sources].add(d_joined[:, :width])  8.81 us
    dot_general x4, matrix products, left_dot(): lax.dot_general(first, second, (((0,), (0,)), ((), ())), preferred_elemen...  6.67 us
  transfers between devices with their start and end apart: 9, of which 4 were waited for; matrix products, arithmetic and copies ran while one was open for 21% of the time, Pallas kernels for 0%

profile of v1, /device:TPU:8, one launch (start us, length us, event | category | flops | bytes accessed | tf_op | source)
XLA Modules:
  0.0 276.5 jit_solution(17933292323248175010)
XLA Ops:
  7.2 1.1 fusion.41
  8.3 1.3 collective-permute-start.1
  9.6 4.6 %collective-permute-start = (bf16[128,512]{1,0:T(8,128)(2,1)S(1)}, bf16[128,512]{1,0:T(8,128)(2,1)S(1)}, u32[]{:S(2)}, u32[]{:S(2)}) collective-permute-start(bf16[128,512]{1,0:T(8,128)(2,1)S(1)} %get-tuple-element.57), channel_id=1, source_target_pairs={{0,1},{1,2},{2,3},{3,4},{4,5},{5,6},{6,7},{7,8},{8,9},{9,10},{10,1... | collective-permute-start | bytes 393224 | tf_op jit(solution)/shard_map/ppermute | solution.py:16
  14.8 0.7 broadcast_multiply_fusion.3
  15.4 0.8 compare_select_fusion.1
  16.2 1.4 copy.25
  17.8 4.0 %gather_fusion.1 = bf16[1024,512]{1,0:T(8,128)(2,1)S(1)} fusion(bf16[1024,512]{1,0:T(8,128)(2,1)S(1)} %constant_dynamic-update-slice_fusion, s32[1024]{0:T(1024)S(1)} %get-tuple-element.70), kind=kCustom, calls=%fused_computation.1 | custom fusion | bytes 2101248 | tf_op jit(solution)/shard_map/gather | solution.py:78
  21.8 5.1 %gather_fusion = bf16[1024,512]{1,0:T(8,128)(2,1)} fusion(bf16[1024,512]{1,0:T(8,128)(2,1)S(1)} %constant_dynamic-update-slice_fusion, s32[1024]{0:T(1024)S(1)} %get-tuple-element.59), kind=kCustom, calls=%fused_computation | custom fusion | bytes 2101248 | tf_op jit(solution)/shard_map/gather | solution.py:78
  26.8 1.4 constant_dynamic-update-slice_fusion.5
  28.5 1.9 copy-done.10
  30.3 3.4 %multiply_convert_fusion.2 = (bf16[1024,512]{1,0:T(8,128)(2,1)S(1)}, f32[1024,512]{1,0:T(8,128)}) fusion(bf16[1024,1536]{1,0:T(8,128)(2,1)S(1)} %constant_dynamic-update-slice_fusion.3, bf16[3584,512]{1,0:T(8,128)(2,1)S(1)} %copy-done.10), kind=kOutput, calls=%fused_computation.25 | convolution fusion | flops 1613234176 | bytes 7864320 | tf_op jit(solution)/shard_map/dot_general | solution.py:79
  33.7 0.8 fusion.42
  34.5 0.4 multiply_reduce_fusion.1
  34.9 0.5 multiply_convert_fusion.1
  35.4 0.2 copy-done.14
  35.6 2.2 fusion.21
  37.8 1.4 broadcast_in_dim.43
  39.2 4.9 %scatter_fusion = f32[6,128,512]{2,1,0:T(8,128)} fusion(f32[6,128,512]{2,1,0:T(8,128)} %broadcast_in_dim.43, s32[8]{0:T(128)S(1)} %get-tuple-element.63, f32[8,128,512]{2,1,0:T(8,128)} %fusion.21), kind=kCustom, calls=%fused_computation.3 | custom fusion | flops 524288 | bytes 6291488 | tf_op jit(solution)/shard_map/scatter-add | solution.py:92
  44.1 1.6 convert_element_type.62
  45.7 2.3 fusion.15
  48.0 0.7 fusion.43
  48.8 0.3 multiply_reduce_fusion.2
  49.2 0.4 fusion.19
  49.6 0.4 add_convert_fusion.1
  50.0 0.9 multiply_convert_fusion.3
  50.9 1.6 fusion.38
  52.6 2.4 fusion.14
  54.9 1.0 fusion.16
  56.0 1.7 copy-done
  57.7 1.0 slice.162
  58.7 2.7 gather_fusion.2
  61.4 1.8 fusion.20
  63.2 0.8 multiply_reduce_fusion
  64.1 1.6 fusion.39
  65.7 0.8 fusion.37
  66.5 0.8 copy-done.17
  67.3 2.4 multiply_convert_fusion
  69.7 1.0 copy-done.16
  70.7 1.9 fusion.44
  72.6 1.0 pad_maximum_fusion
  73.6 4.1 %copy.30 = f32[2,4,2,224,512]{4,3,0,1,2:T(8,128)} copy(f32[2,4,2,224,512]{4,3,2,1,0:T(8,128)S(1)} %bitcast.40) | data formatting | bytes 14680064 | tf_op jit(solution)/shard_map/reshape | solution.py:134
  77.8 28.6 %reduce-scatter.7.cloned.1.call-done = f32[1792,512]{1,0:T(8,128)} async-done(((f32[3584,512]{1,0:T(8,128)}), f32[1792,512]{1,0:T(8,128)}) %reduce-scatter.7.cloned.1.call-update) | async-done | bytes 3670032 | tf_op jit(solution)/shard_map/reduce_scatter | solution.py:138
  106.5 47.7 %reduce-scatter.9.cloned.1.call-done = f32[448,512]{1,0:T(8,128)} async-done(((f32[1792,512]{1,0:T(8,128)}), f32[448,512]{1,0:T(8,128)}) %reduce-scatter.9.cloned.1.call-update) | async-done | bytes 917520 | tf_op jit(solution)/shard_map/reduce_scatter | solution.py:138
  154.2 0.6 dynamic-slice.28
  155.5 1.7 copy.33
  157.2 6.2 %fusion.9 = f32[1024,1536]{1,0:T(8,128)} fusion(bf16[1024,512]{1,0:T(8,128)(2,1)} %copy-done.16, bf16[3584,512]{1,0:T(8,128)(2,1)} %param.23), kind=kOutput, calls=%fused_computation.36 | convolution fusion | flops 1610612736 | bytes 8912896 | tf_op jit(solution)/shard_map/dot_general | solution.py:57
  163.4 8.8 %scatter_custom_fusion.1 = f32[1024,512]{1,0:T(8,128)} fusion(s32[1024]{0:T(1024)S(1)} %get-tuple-element.58, f32[1024,1536]{1,0:T(8,128)} %fusion.9, f32[]{:T(128)} %constant.111.clone.1), kind=kCustom, calls=%fused_computation.18 | custom fusion | flops 524288 | bytes 4194816 | tf_op jit(solution)/shard_map/scatter-add | solution.py:117
  172.2 10.3 %scatter_custom_fusion.2 = f32[1024,512]{1,0:T(8,128)} fusion(f32[1024,512]{1,0:T(8,128)} %scatter_custom_fusion.1, s32[1024]{0:T(1024)S(1)} %get-tuple-element.71, f32[1024,1536]{1,0:T(8,128)} %fusion.9), kind=kCustom, calls=%fused_computation.16 | custom fusion | flops 524288 | bytes 4194304 | tf_op jit(solution)/shard_map/scatter-add | solution.py:118
  182.5 1.9 copy.27
  184.6 3.4 %collective-permute-start.2 = (bf16[128,512]{0,1:T(8,128)(2,1)S(1)}, bf16[128,512]{0,1:T(8,128)(2,1)S(1)}, u32[]{:S(2)}, u32[]{:S(2)}) collective-permute-start(bf16[128,512]{0,1:T(8,128)(2,1)S(1)} %get-tuple-element.55), channel_id=1, source_target_pairs={{0,1},{1,2},{2,3},{3,4},{4,5},{5,6},{6,7},{7,8},{8,9},{9,10},{10,1... | collective-permute-start | bytes 393224 | tf_op jit(solution)/shard_map/ppermute | solution.py:31
  188.1 8.2 %reduce-scatter.11.cloned.1.call-done = f32[224,512]{1,0:T(8,128)} async-done(((f32[448,512]{1,0:T(8,128)}), f32[224,512]{1,0:T(8,128)}) %reduce-scatter.11.cloned.1.call-update) | async-done | bytes 458768 | tf_op jit(solution)/shard_map/reduce_scatter | solution.py:138
  196.3 2.9 %fusion.8 = f32[768,512]{0,1:T(8,128)} fusion(f32[768,512]{0,1:T(8,128)} %copy.33, bf16[768,512]{0,1:T(8,128)(2,1)S(1)} %copy.25, f32[1024,512]{0,1:T(8,128)S(1)} %copy.27), kind=kLoop, calls=%fused_computation.28 | loop fusion | flops 1179648 | bytes 5505024 | tf_op jit(solution)/shard_map/add | solution.py:119
  199.2 2.9 %fusion.2 = bf16[1024,512]{1,0:T(8,128)(2,1)} fusion(bf16[1024,512]{1,0:T(8,128)(2,1)S(1)} %copy-done.2, f32[1024,1536]{1,0:T(8,128)} %fusion.9), kind=kLoop, calls=%fused_computation.15 | loop fusion | flops 1572864 | bytes 4194304 | tf_op jit(solution)/shard_map/convert_element_type | solution.py:115
  202.1 1.3 collective-permute-start.3
  203.4 1.7 fusion.29
  205.1 17.2 %reduce-scatter.13.cloned.1.call-done = f32[56,512]{1,0:T(8,128)} async-done(((f32[224,512]{1,0:T(8,128)}), f32[56,512]{1,0:T(8,128)}) %reduce-scatter.13.cloned.1.call-update) | async-done | bytes 114704 | tf_op jit(solution)/shard_map/reduce_scatter | solution.py:138
  222.3 12.6 %fusion = f32[16,512]{1,0:T(8,128)S(1)} fusion(f32[56,512]{1,0:T(8,128)} %reduce-scatter.13.cloned.1.call-done), kind=kCustom, calls=%all-reduce-scatter | all-reduce-scatter fusion | flops 32769 | bytes 148480
  234.9 3.1 %collective-permute-start.4 = (f32[6,512]{1,0:T(8,128)S(1)}, f32[6,512]{1,0:T(8,128)S(1)}, u32[]{:S(2)}, u32[]{:S(2)}) collective-permute-start(f32[6,512]{1,0:T(8,128)S(1)} %slice.132), channel_id=1, source_target_pairs={{0,4},{4,8},{8,12},{1,5},{5,9},{9,13},{2,6},{6,10},{10,14},{3,7},{... | collective-permute-start | bytes 36872
  238.1 1.7 fusion.28
  239.8 1.5 convert_element_type.72
  241.3 1.2 copy.31
  242.6 12.0 %all-gather = f32[4,14,512]{2,1,0:T(8,128)S(1)} all-gather(f32[1,14,512]{2,1,0:T(8,128)S(1)} %dynamic-slice_bitcast_fusion), channel_id=1, replica_groups=mesh['zh'=2,'y'=4,'c'=2,'x'=4,'zl'=4] {'x'}, dimensions={0}, use_global_device_ids=true | all-gather | bytes 143360 | tf_op jit(solution)/shard_map/all_gather | solution.py:140
  254.6 14.6 %all_gather.7 = f32[224,512]{1,0:T(8,128)S(1)} all-gather(f32[56,512]{1,0:T(8,128)S(1)} %reshape.212), channel_id=1, replica_groups=mesh['zh'=2,'y'=4,'c'=2,'x'=4,'zl'=4] {'zl'}, dimensions={0}, use_global_device_ids=true | all-gather | bytes 573440 | tf_op jit(solution)/shard_map/all_gather | solution.py:140
  269.2 0.8 broadcast_multiply_fusion
  (66 shorter events, 1.0 us)
Async XLA Ops:
  7.2 10.5 %copy-start.4 = (bf16[768,512]{1,0:T(8,128)(2,1)S(1)}, bf16[768,512]{1,0:T(8,128)(2,1)}, u32[]{:S(2)}) copy-start(bf16[768,512]{1,0:T(8,128)(2,1)} %param.15) | copy-start | bytes 2359300
  7.2 99.2 %reduce-scatter.7.cloned.1.call-start = ((), (), s32[]{:S(2)}) async-start(), calls=%async_computation.4 | async-start | bytes 11010048 | tf_op jit(solution)/shard_map/reduce_scatter | solution.py:138
  8.3 9.5 %collective-permute-start.1 = (bf16[128,512]{1,0:T(8,128)(2,1)S(1)}, bf16[128,512]{1,0:T(8,128)(2,1)S(1)}, u32[]{:S(2)}, u32[]{:S(2)}) collective-permute-start(bf16[128,512]{1,0:T(8,128)(2,1)S(1)} %get-tuple-element.56), channel_id=1, source_target_pairs={{1,0},{2,1},{3,2},{4,3},{5,4},{6,5},{7,6},{8,7},{9,8},{10,9},{11,1... | collective-permute-start | bytes 393224 | tf_op jit(solution)/shard_map/ppermute | solution.py:19
  9.6 8.1 %collective-permute-start = (bf16[128,512]{1,0:T(8,128)(2,1)S(1)}, bf16[128,512]{1,0:T(8,128)(2,1)S(1)}, u32[]{:S(2)}, u32[]{:S(2)}) collective-permute-start(bf16[128,512]{1,0:T(8,128)(2,1)S(1)} %get-tuple-element.57), channel_id=1, source_target_pairs={{0,1},{1,2},{2,3},{3,4},{4,5},{5,6},{6,7},{7,8},{8,9},{9,10},{10,1... | collective-permute-start | bytes 393224 | tf_op jit(solution)/shard_map/ppermute | solution.py:16
  26.8 1.5 copy-start.7
  28.2 2.1 copy-start.10
  30.3 3.4 %copy-start.12 = (bf16[1024,1536]{1,0:T(8,128)(2,1)}, bf16[1024,1536]{1,0:T(8,128)(2,1)S(1)}, u32[]{:S(2)}) copy-start(bf16[1024,1536]{1,0:T(8,128)(2,1)S(1)} %constant_dynamic-update-slice_fusion.3) | copy-start | bytes 9437188
  33.7 1.2 copy-start.8
  34.9 0.7 copy-start.14
  44.1 1.6 copy-start.5
  45.7 2.4 copy-start.11
  56.0 1.8 copy-start
  61.4 1.8 copy-start.1
  64.1 1.6 copy-start.9
  65.7 1.6 copy-start.17
  67.3 3.4 %copy-start.13 = (bf16[1024,1536]{1,0:T(8,128)(2,1)S(1)}, bf16[1024,1536]{1,0:T(8,128)(2,1)}, u32[]{:S(2)}) copy-start(bf16[1024,1536]{1,0:T(8,128)(2,1)} %copy-done.12) | copy-start | bytes 9437188
  69.7 1.0 copy-start.16
  70.7 1.9 copy-start.3
  70.7 1.9 copy-start.6
  77.7 76.4 %reduce-scatter.9.cloned.1.call-start = ((), (), s32[]{:S(2)}) async-start(), calls=%async_computation.5 | async-start | bytes 4587520 | tf_op jit(solution)/shard_map/reduce_scatter | solution.py:138
  106.4 47.8 %copy-start.15 = (u32[256]{0:T(256)S(1)}, u32[256]{0:T(256)}, u32[]{:S(2)}) copy-start(u32[256]{0:T(256)} %constant.126) | copy-start | bytes 3076
  106.4 49.0 %slice-start = ((f32[768,1024]{1,0:T(8,128)}), f32[768,512]{1,0:T(8,128)S(1)}, s32[]{:S(2)}) async-start(f32[768,1024]{1,0:T(8,128)} %copy-done), calls=%async_computation.8 | async-start | bytes 3145728 | tf_op jit(solution)/shard_map/slice | solution.py:120
  106.4 89.8 %reduce-scatter.11.cloned.1.call-start = ((), (), s32[]{:S(2)}) async-start(), calls=%async_computation.6 | async-start | bytes 1376256 | tf_op jit(solution)/shard_map/reduce_scatter | solution.py:138
  154.2 68.1 %reduce-scatter.13.cloned.1.call-start = ((), (), s32[]{:S(2)}) async-start(), calls=%async_computation.7 | async-start | bytes 573440 | tf_op jit(solution)/shard_map/reduce_scatter | solution.py:138
  184.6 18.7 %collective-permute-start.2 = (bf16[128,512]{0,1:T(8,128)(2,1)S(1)}, bf16[128,512]{0,1:T(8,128)(2,1)S(1)}, u32[]{:S(2)}, u32[]{:S(2)}) collective-permute-start(bf16[128,512]{0,1:T(8,128)(2,1)S(1)} %get-tuple-element.55), channel_id=1, source_target_pairs={{0,1},{1,2},{2,3},{3,4},{4,5},{5,6},{6,7},{7,8},{8,9},{9,10},{10,1... | collective-permute-start | bytes 393224 | tf_op jit(solution)/shard_map/ppermute | solution.py:31
  196.3 2.9 %copy-start.2 = (bf16[1024,512]{1,0:T(8,128)(2,1)S(1)}, bf16[1024,512]{1,0:T(8,128)(2,1)}, u32[]{:S(2)}) copy-start(bf16[1024,512]{1,0:T(8,128)(2,1)} %param.18) | copy-start | bytes 3145732
  202.1 36.0 %collective-permute-start.3 = (bf16[128,512]{0,1:T(8,128)(2,1)S(1)}, bf16[128,512]{0,1:T(8,128)(2,1)S(1)}, u32[]{:S(2)}, u32[]{:S(2)}) collective-permute-start(bf16[128,512]{0,1:T(8,128)(2,1)S(1)} %get-tuple-element.54), channel_id=1, source_target_pairs={{1,0},{2,1},{3,2},{4,3},{5,4},{6,5},{7,6},{8,7},{9,8},{10,9},{11,1... | collective-permute-start | bytes 393224 | tf_op jit(solution)/shard_map/ppermute | solution.py:31
  234.9 7.5 %collective-permute-start.4 = (f32[6,512]{1,0:T(8,128)S(1)}, f32[6,512]{1,0:T(8,128)S(1)}, u32[]{:S(2)}, u32[]{:S(2)}) collective-permute-start(f32[6,512]{1,0:T(8,128)S(1)} %slice.132), channel_id=1, source_target_pairs={{0,4},{4,8},{8,12},{1,5},{5,9},{9,13},{2,6},{6,10},{10,14},{3,7},{... | collective-permute-start | bytes 36872
Sparse Core Ops, SparseCore 0:
  77.9 28.5 reduce-scatter.6
  109.0 45.1 reduce-scatter.8
  156.7 39.5 reduce-scatter.10
  198.7 23.6 reduce-scatter.12

commit v2 on v1

--- a/solution.py
+++ b/solution.py
@@ -128,15 +128,17 @@
 
 
 def reduce_grads(grads):
-    sizes = [lax.axis_size(name) for name in DP]
+    gather = ("x", "zl")
+    dims = DP + (gather[1], gather[0])
+    sizes = [lax.axis_size(name) for name in dims]
     rows = grads.shape[0] // int(np.prod(sizes))
-    order = ("c", "y", "zh")
+    order = ("c", "y", "x", "zl", "zh")
     blocks = grads.reshape(*sizes, rows, grads.shape[1])
-    blocks = blocks.transpose([DP.index(name) for name in order] + [3, 4])
+    blocks = blocks.transpose([dims.index(name) for name in order] + [5, 6])
     part = blocks.reshape(grads.shape)
-    for name in order + ("zl", "x"):
+    for name in order:
         part = lax.psum_scatter(part, name, scatter_dimension=0, tiled=True)
-    for name in ("x", "zl"):
+    for name in gather:
         part = lax.all_gather(part, name, axis=0, tiled=True)
     return part
 

time: 278 us -> 300 us (1.079)
  waiting for transfers between devices: 102 us -> 76.4 us
  local copies, waits for them, and re-layouts: 33.7 us -> 56.8 us
  blocking collectives: 39.1 us -> 57.2 us
  starting transfers between devices: 13.9 us -> 18.4 us
    reduce_scatter x4 -> x3, waiting for transfers between devices: 102 us -> 76.3 us  [reduce_grads(): part = lax.psum_scatter(part, name, scatter_dimension=0, tiled=True)]
    unnamed x1 -> x2, blocking collectives: 12.6 us -> 30.4 us
    reshape x0 -> x1, local copies, waits for them, and re-layouts: none -> 9.08 us  [reduce_grads(): part = blocks.reshape(grads.shape)]
    transpose x0 -> x1, local copies, waits for them, and re-layouts: none -> 8.51 us  [reduce_grads(): blocks = blocks.transpose([dims.index(name) for name in order] + [5, 6])]
    reshape x1, local copies, waits for them, and re-layouts: 4.13 us -> 9 us  [reduce_grads(): blocks = grads.reshape(*sizes, rows, grads.shape[1])]
    unnamed x1 -> x2, starting transfers between devices: 3.14 us -> 6.33 us
    unnamed x48 -> x56, local copies, waits for them, and re-layouts: 12.2 us -> 12.9 us
  transfers between devices with their start and end apart: 9 -> 9, of which waited for: 4 -> 2; matrix products, arithmetic and copies ran while one was open for 21% -> 25% of each run, Pallas kernels for 0% -> 0%
where the time goes in v2:
time: 300 us; the launch traced here: 299 us
  waiting for transfers between devices  76.4 us (25%)
  blocking collectives  57.2 us (19%)
  local copies, waits for them, and re-layouts  56.8 us (19%)
  other arithmetic  45 us (15%)
  matrix products  28.4 us (9%)
  starting transfers between devices  18.4 us (6%)
  between operations  16.2 us (5%)
    reduce_scatter x3, waiting for transfers between devices, reduce_grads(): part = lax.psum_scatter(part, name, scatter_dimension=0, tiled=True)  76.3 us
    unnamed x2, blocking collectives  30.4 us
    all_gather x2, blocking collectives, reduce_grads(): part = lax.all_gather(part, name, axis=0, tiled=True)  26.9 us
    unnamed x56, local copies, waits for them, and re-layouts  12.9 us
    dot_general x4, matrix products, right_dot(): lax.dot_general(first, second, (((1,), (1,)), ((), ())), preferred_elemen...  10.6 us
    scatter-add x1, other arithmetic, slab_backward(): d_extended = d_extended.at[dest + rim].add(d_joined[:, width:2 * width])  10.3 us
    reshape x1, local copies, waits for them, and re-layouts, reduce_grads(): part = blocks.reshape(grads.shape)  9.08 us
    reshape x1, local copies, waits for them, and re-layouts, reduce_grads(): blocks = grads.reshape(*sizes, rows, grads.shape[1])  9 us
  transfers between devices with their start and end apart: 9, of which 2 were waited for; matrix products, arithmetic and copies ran while one was open for 25% of the time, Pallas kernels for 0%

profile of v2, /device:TPU:8, one launch (start us, length us, event | category | flops | bytes accessed | tf_op | source)
XLA Modules:
  0.0 298.5 jit_solution(2231849798750489595)
XLA Ops:
  7.2 1.1 fusion.42
  8.3 1.3 collective-permute-start.1
  9.6 4.6 %collective-permute-start = (bf16[128,512]{1,0:T(8,128)(2,1)S(1)}, bf16[128,512]{1,0:T(8,128)(2,1)S(1)}, u32[]{:S(2)}, u32[]{:S(2)}) collective-permute-start(bf16[128,512]{1,0:T(8,128)(2,1)S(1)} %get-tuple-element.57), channel_id=1, source_target_pairs={{0,1},{1,2},{2,3},{3,4},{4,5},{5,6},{6,7},{7,8},{8,9},{9,10},{10,1... | collective-permute-start | bytes 393224 | tf_op jit(solution)/shard_map/ppermute | solution.py:16
  14.8 0.7 broadcast_multiply_fusion.3
  15.4 0.8 compare_select_fusion.1
  16.2 1.4 copy.25
  17.8 4.0 %gather_fusion.1 = bf16[1024,512]{1,0:T(8,128)(2,1)S(1)} fusion(bf16[1024,512]{1,0:T(8,128)(2,1)S(1)} %constant_dynamic-update-slice_fusion, s32[1024]{0:T(1024)S(1)} %get-tuple-element.70), kind=kCustom, calls=%fused_computation.1 | custom fusion | bytes 2101248 | tf_op jit(solution)/shard_map/gather | solution.py:78
  21.8 5.1 %gather_fusion = bf16[1024,512]{1,0:T(8,128)(2,1)} fusion(bf16[1024,512]{1,0:T(8,128)(2,1)S(1)} %constant_dynamic-update-slice_fusion, s32[1024]{0:T(1024)S(1)} %get-tuple-element.59), kind=kCustom, calls=%fused_computation | custom fusion | bytes 2101248 | tf_op jit(solution)/shard_map/gather | solution.py:78
  26.8 1.4 constant_dynamic-update-slice_fusion.5
  28.5 1.9 copy-done.11
  30.3 3.4 %multiply_convert_fusion.2 = (bf16[1024,512]{1,0:T(8,128)(2,1)S(1)}, f32[1024,512]{1,0:T(8,128)}) fusion(bf16[1024,1536]{1,0:T(8,128)(2,1)S(1)} %constant_dynamic-update-slice_fusion.3, bf16[3584,512]{1,0:T(8,128)(2,1)S(1)} %copy-done.11), kind=kOutput, calls=%fused_computation.25 | convolution fusion | flops 1613234176 | bytes 7864320 | tf_op jit(solution)/shard_map/dot_general | solution.py:79
  33.7 0.8 fusion.43
  34.5 0.4 multiply_reduce_fusion.1
  34.9 0.5 multiply_convert_fusion.1
  35.6 2.2 fusion.22
  37.8 1.4 broadcast_in_dim.43
  39.2 4.8 %scatter_fusion = f32[6,128,512]{2,1,0:T(8,128)} fusion(f32[6,128,512]{2,1,0:T(8,128)} %broadcast_in_dim.43, s32[8]{0:T(128)S(1)} %get-tuple-element.63, f32[8,128,512]{2,1,0:T(8,128)} %fusion.22), kind=kCustom, calls=%fused_computation.3 | custom fusion | flops 524288 | bytes 6291488 | tf_op jit(solution)/shard_map/scatter-add | solution.py:92
  44.0 1.6 convert_element_type.62
  45.6 2.3 fusion.16
  48.0 0.7 fusion.44
  49.5 0.4 add_convert_fusion.1
  49.9 1.0 multiply_convert_fusion.3
  50.8 1.6 fusion.39
  52.5 2.4 fusion.15
  54.8 1.0 fusion.17
  55.9 1.7 copy-done
  57.5 1.0 slice.163
  58.5 2.7 gather_fusion.2
  61.2 1.8 fusion.21
  63.0 0.8 multiply_reduce_fusion
  63.9 1.6 fusion.40
  65.5 0.8 fusion.38
  66.3 0.8 copy-done.19
  67.1 2.4 multiply_convert_fusion
  69.5 1.0 copy-done.18
  70.5 1.9 fusion.45
  72.4 3.4 %pad_maximum_fusion = f32[3584,512]{1,0:T(8,128)} fusion(f32[512,512]{1,0:T(8,128)S(1)} %copy-done.7, f32[1024,512]{1,0:T(8,128)S(1)} %copy-done.4, f32[512,512]{1,0:T(8,128)S(1)} %fusion.38, f32[1536,512]{1,0:T(8,128)S(1)} %fusion.45), kind=kLoop, calls=%fused_computation.6 | loop fusion | flops 5505024 | bytes 14680064 | tf_op jit(solution)/shard_map/concatenate | solution.py:122
  75.8 9.0 %reshape.155 = f32[2,4,2,4,4,14,512]{6,5,4,3,2,1,0:T(8,128)} reshape(f32[3584,512]{1,0:T(8,128)} %pad_maximum_fusion) | data formatting | bytes 14680064 | tf_op jit(solution)/shard_map/reshape | solution.py:136
  84.8 8.5 %copy.30 = f32[2,4,4,4,2,14,512]{6,5,4,3,2,1,0:T(8,128)} copy(f32[2,4,4,4,2,14,512]{6,5,2,3,0,1,4:T(8,128)} %bitcast.39) | data formatting | bytes 14680064 | tf_op jit(solution)/shard_map/transpose | solution.py:137
  93.3 9.1 %reshape.156 = f32[3584,512]{1,0:T(8,128)} reshape(f32[2,4,4,4,2,14,512]{6,5,4,3,2,1,0:T(8,128)} %copy.30) | data formatting | bytes 14680064 | tf_op jit(solution)/shard_map/reshape | solution.py:138
  102.5 28.6 %reduce-scatter.8.cloned.1.call-done = f32[1792,512]{1,0:T(8,128)} async-done(((f32[3584,512]{1,0:T(8,128)}), f32[1792,512]{1,0:T(8,128)}) %reduce-scatter.8.cloned.1.call-update) | async-done | bytes 3670032 | tf_op jit(solution)/shard_map/reduce_scatter | solution.py:140
  131.2 47.7 %reduce-scatter.10.cloned.1.call-done = f32[448,512]{1,0:T(8,128)} async-done(((f32[1792,512]{1,0:T(8,128)}), f32[448,512]{1,0:T(8,128)}) %reduce-scatter.10.cloned.1.call-update) | async-done | bytes 917520 | tf_op jit(solution)/shard_map/reduce_scatter | solution.py:140
  178.9 0.6 dynamic-slice.34
  180.1 0.6 dynamic-slice.30
  181.4 1.7 copy.33
  183.1 6.2 %fusion.10 = f32[1024,1536]{1,0:T(8,128)} fusion(bf16[1024,512]{1,0:T(8,128)(2,1)} %copy-done.18, bf16[3584,512]{1,0:T(8,128)(2,1)} %param.23), kind=kOutput, calls=%fused_computation.36 | convolution fusion | flops 1610612736 | bytes 8912896 | tf_op jit(solution)/shard_map/dot_general | solution.py:57
  189.3 8.8 %scatter_custom_fusion.1 = f32[1024,512]{1,0:T(8,128)} fusion(s32[1024]{0:T(1024)S(1)} %get-tuple-element.58, f32[1024,1536]{1,0:T(8,128)} %fusion.10, f32[]{:T(128)} %constant.111.clone.1), kind=kCustom, calls=%fused_computation.18 | custom fusion | flops 524288 | bytes 4194816 | tf_op jit(solution)/shard_map/scatter-add | solution.py:117
  198.1 10.3 %scatter_custom_fusion.2 = f32[1024,512]{1,0:T(8,128)} fusion(f32[1024,512]{1,0:T(8,128)} %scatter_custom_fusion.1, s32[1024]{0:T(1024)S(1)} %get-tuple-element.71, f32[1024,1536]{1,0:T(8,128)} %fusion.10), kind=kCustom, calls=%fused_computation.16 | custom fusion | flops 524288 | bytes 4194304 | tf_op jit(solution)/shard_map/scatter-add | solution.py:118
  208.4 1.9 copy.27
  210.6 1.4 collective-permute-start.3
  212.0 4.7 %collective-permute-start.2 = (bf16[128,512]{0,1:T(8,128)(2,1)S(1)}, bf16[128,512]{0,1:T(8,128)(2,1)S(1)}, u32[]{:S(2)}, u32[]{:S(2)}) collective-permute-start(bf16[128,512]{0,1:T(8,128)(2,1)S(1)} %get-tuple-element.55), channel_id=1, source_target_pairs={{0,1},{1,2},{2,3},{3,4},{4,5},{5,6},{6,7},{7,8},{8,9},{9,10},{10,1... | collective-permute-start | bytes 393224 | tf_op jit(solution)/shard_map/ppermute | solution.py:31
  216.7 2.9 fusion.3
  219.6 1.4 fusion.9
  221.1 18.2 %fusion = f32[32,512]{1,0:T(8,128)S(1)} fusion(f32[112,512]{1,0:T(8,128)} %reduce-scatter.12.cloned.1.call-done), kind=kCustom, calls=%all-reduce-scatter | all-reduce-scatter fusion | flops 65537 | bytes 295936
  239.3 1.3 collective-permute-start.4
  240.6 1.7 fusion.30
  242.5 12.2 %fusion.1 = f32[16,512]{1,0:T(8,128)S(1)} fusion(f32[28,512]{1,0:T(8,128)S(1)} %constant_dynamic-slice_fusion), kind=kCustom, calls=%all-reduce-scatter.1 | all-reduce-scatter fusion | flops 16385 | bytes 91136
  254.7 5.0 %collective-permute-start.5 = (f32[2,512]{1,0:T(2,128)S(1)}, f32[2,512]{1,0:T(2,128)S(1)}, u32[]{:S(2)}, u32[]{:S(2)}) collective-permute-start(f32[2,512]{1,0:T(2,128)S(1)} %slice.133), channel_id=1, source_target_pairs={{0,128},{1,129},{2,130},{3,131},{4,132},{5,133},{6,134},{7,135},{8... | collective-permute-start | bytes 12296
  259.8 1.7 fusion.29
  261.5 1.5 convert_element_type.72
  263.0 1.2 copy.31
  264.3 12.2 %all-gather = f32[4,14,512]{2,1,0:T(8,128)S(1)} all-gather(f32[1,14,512]{2,1,0:T(8,128)S(1)} %dynamic-slice_bitcast_fusion), channel_id=1, replica_groups=mesh['zh'=2,'y'=4,'c'=2,'x'=4,'zl'=4] {'x'}, dimensions={0}, use_global_device_ids=true | all-gather | bytes 143360 | tf_op jit(solution)/shard_map/all_gather | solution.py:142
  276.6 14.6 %all_gather.7 = f32[224,512]{1,0:T(8,128)S(1)} all-gather(f32[56,512]{1,0:T(8,128)S(1)} %reshape.212), channel_id=1, replica_groups=mesh['zh'=2,'y'=4,'c'=2,'x'=4,'zl'=4] {'zl'}, dimensions={0}, use_global_device_ids=true | all-gather | bytes 573440 | tf_op jit(solution)/shard_map/all_gather | solution.py:142
  291.2 0.8 broadcast_multiply_fusion
  (76 shorter events, 2.1 us)
Async XLA Ops:
  7.2 10.5 %copy-start.5 = (bf16[768,512]{1,0:T(8,128)(2,1)S(1)}, bf16[768,512]{1,0:T(8,128)(2,1)}, u32[]{:S(2)}) copy-start(bf16[768,512]{1,0:T(8,128)(2,1)} %param.15) | copy-start | bytes 2359300
  7.2 123.9 %reduce-scatter.8.cloned.1.call-start = ((), (), s32[]{:S(2)}) async-start(), calls=%async_computation.3 | async-start | bytes 11010048 | tf_op jit(solution)/shard_map/reduce_scatter | solution.py:140
  8.3 9.5 %collective-permute-start.1 = (bf16[128,512]{1,0:T(8,128)(2,1)S(1)}, bf16[128,512]{1,0:T(8,128)(2,1)S(1)}, u32[]{:S(2)}, u32[]{:S(2)}) collective-permute-start(bf16[128,512]{1,0:T(8,128)(2,1)S(1)} %get-tuple-element.56), channel_id=1, source_target_pairs={{1,0},{2,1},{3,2},{4,3},{5,4},{6,5},{7,6},{8,7},{9,8},{10,9},{11,1... | collective-permute-start | bytes 393224 | tf_op jit(solution)/shard_map/ppermute | solution.py:19
  9.6 8.1 %collective-permute-start = (bf16[128,512]{1,0:T(8,128)(2,1)S(1)}, bf16[128,512]{1,0:T(8,128)(2,1)S(1)}, u32[]{:S(2)}, u32[]{:S(2)}) collective-permute-start(bf16[128,512]{1,0:T(8,128)(2,1)S(1)} %get-tuple-element.57), channel_id=1, source_target_pairs={{0,1},{1,2},{2,3},{3,4},{4,5},{5,6},{6,7},{7,8},{8,9},{9,10},{10,1... | collective-permute-start | bytes 393224 | tf_op jit(solution)/shard_map/ppermute | solution.py:16
  26.8 1.5 copy-start.8
  28.2 2.1 copy-start.11
  30.3 3.4 %copy-start.13 = (bf16[1024,1536]{1,0:T(8,128)(2,1)}, bf16[1024,1536]{1,0:T(8,128)(2,1)S(1)}, u32[]{:S(2)}) copy-start(bf16[1024,1536]{1,0:T(8,128)(2,1)S(1)} %constant_dynamic-update-slice_fusion.3) | copy-start | bytes 9437188
  33.7 1.2 copy-start.9
  34.9 0.7 copy-start.15
  44.0 1.6 copy-start.6
  45.6 2.4 copy-start.12
  55.8 1.7 copy-start
  61.2 1.8 copy-start.1
  63.9 1.6 copy-start.10
  65.5 1.6 copy-start.19
  67.1 3.4 %copy-start.14 = (bf16[1024,1536]{1,0:T(8,128)(2,1)S(1)}, bf16[1024,1536]{1,0:T(8,128)(2,1)}, u32[]{:S(2)}) copy-start(bf16[1024,1536]{1,0:T(8,128)(2,1)} %copy-done.13) | copy-start | bytes 9437188
  69.5 1.0 copy-start.18
  70.5 1.9 copy-start.4
  70.5 1.9 copy-start.7
  102.4 76.4 %reduce-scatter.10.cloned.1.call-start = ((), (), s32[]{:S(2)}) async-start(), calls=%async_computation.4 | async-start | bytes 4587520 | tf_op jit(solution)/shard_map/reduce_scatter | solution.py:140
  131.1 47.8 %copy-start.17 = (u32[256]{0:T(256)S(1)}, u32[256]{0:T(256)}, u32[]{:S(2)}) copy-start(u32[256]{0:T(256)} %constant.130) | copy-start | bytes 3076
  131.1 49.0 %copy-start.16 = (u32[256]{0:T(256)S(1)}, u32[256]{0:T(256)}, u32[]{:S(2)}) copy-start(u32[256]{0:T(256)} %constant.126) | copy-start | bytes 3076
  131.1 50.2 %slice-start = ((f32[768,1024]{1,0:T(8,128)}), f32[768,512]{1,0:T(8,128)S(1)}, s32[]{:S(2)}) async-start(f32[768,1024]{1,0:T(8,128)} %copy-done), calls=%async_computation.6 | async-start | bytes 3145728 | tf_op jit(solution)/shard_map/slice | solution.py:120
  131.1 89.9 %reduce-scatter.12.cloned.1.call-start = ((), (), s32[]{:S(2)}) async-start(), calls=%async_computation.5 | async-start | bytes 1146880 | tf_op jit(solution)/shard_map/reduce_scatter | solution.py:140
  210.3 6.4 %copy-start.2 = (bf16[1024,512]{1,0:T(8,128)(2,1)S(1)}, bf16[1024,512]{1,0:T(8,128)(2,1)}, u32[]{:S(2)}) copy-start(bf16[1024,512]{1,0:T(8,128)(2,1)} %param.18) | copy-start | bytes 3145732
  210.6 49.2 %collective-permute-start.3 = (bf16[128,512]{0,1:T(8,128)(2,1)S(1)}, bf16[128,512]{0,1:T(8,128)(2,1)S(1)}, u32[]{:S(2)}, u32[]{:S(2)}) collective-permute-start(bf16[128,512]{0,1:T(8,128)(2,1)S(1)} %get-tuple-element.54), channel_id=1, source_target_pairs={{1,0},{2,1},{3,2},{4,3},{5,4},{6,5},{7,6},{8,7},{9,8},{10,9},{11,1... | collective-permute-start | bytes 393224 | tf_op jit(solution)/shard_map/ppermute | solution.py:31
  212.0 7.6 %copy-start.3 = (f32[768,512]{0,1:T(8,128)S(1)}, f32[768,512]{0,1:T(8,128)}, u32[]{:S(2)}) copy-start(f32[768,512]{0,1:T(8,128)} %copy.33) | copy-start | bytes 4718596
  212.0 28.6 %collective-permute-start.2 = (bf16[128,512]{0,1:T(8,128)(2,1)S(1)}, bf16[128,512]{0,1:T(8,128)(2,1)S(1)}, u32[]{:S(2)}, u32[]{:S(2)}) collective-permute-start(bf16[128,512]{0,1:T(8,128)(2,1)S(1)} %get-tuple-element.55), channel_id=1, source_target_pairs={{0,1},{1,2},{2,3},{3,4},{4,5},{5,6},{6,7},{7,8},{8,9},{9,10},{10,1... | collective-permute-start | bytes 393224 | tf_op jit(solution)/shard_map/ppermute | solution.py:31
  239.3 3.0 %collective-permute-start.4 = (f32[12,512]{1,0:T(8,128)S(1)}, f32[12,512]{1,0:T(8,128)S(1)}, u32[]{:S(2)}, u32[]{:S(2)}) collective-permute-start(f32[12,512]{1,0:T(8,128)S(1)} %slice.132), channel_id=1, source_target_pairs={{0,1},{1,2},{2,3},{4,5},{5,6},{6,7},{8,9},{9,10},{10,11},{12,13},{... | collective-permute-start | bytes 73736
  254.7 9.4 %collective-permute-start.5 = (f32[2,512]{1,0:T(2,128)S(1)}, f32[2,512]{1,0:T(2,128)S(1)}, u32[]{:S(2)}, u32[]{:S(2)}) collective-permute-start(f32[2,512]{1,0:T(2,128)S(1)} %slice.133), channel_id=1, source_target_pairs={{0,128},{1,129},{2,130},{3,131},{4,132},{5,133},{6,134},{7,135},{8... | collective-permute-start | bytes 12296
Sparse Core Ops, SparseCore 0:
  102.5 28.5 reduce-scatter.7
  133.7 45.1 reduce-scatter.9
  181.4 26.6 reduce-scatter.11

commit v3 on v1

--- a/solution.py
+++ b/solution.py
@@ -134,9 +134,11 @@
     blocks = grads.reshape(*sizes, rows, grads.shape[1])
     blocks = blocks.transpose([DP.index(name) for name in order] + [3, 4])
     part = blocks.reshape(grads.shape)
-    for name in order + ("zl", "x"):
+    part = lax.psum_scatter(part.astype(jnp.bfloat16), "c", scatter_dimension=0, tiled=True)
+    part = part.astype(jnp.float32)
+    for name in order[1:] + ("x", "zl"):
         part = lax.psum_scatter(part, name, scatter_dimension=0, tiled=True)
-    for name in ("x", "zl"):
+    for name in ("zl", "x"):
         part = lax.all_gather(part, name, axis=0, tiled=True)
     return part
 

time: 278 us -> 267 us (0.960)
  waiting for transfers between devices: 102 us -> 93.3 us
  matrix products: 28.4 us -> 25.4 us
  other arithmetic: 44.1 us -> 47.1 us
    reduce_scatter x4 -> x3, waiting for transfers between devices: 102 us -> 68.8 us  [reduce_grads(): part = lax.psum_scatter(part, name, scatter_dimension=0, tiled=True)]
    reduce_scatter x0 -> x1, waiting for transfers between devices: none -> 24.4 us  [reduce_grads(): lax.psum_scatter(part.astype(jnp.bfloat16), 'c', scatter_dimension=0, til...]
    reshape x1 -> x0, local copies, waits for them, and re-layouts: 4.13 us -> none  [reduce_grads(): blocks = grads.reshape(*sizes, rows, grads.shape[1])]
    convert_element_type x0 -> x1, other arithmetic: none -> 3.81 us  [reduce_grads(): part = part.astype(jnp.float32)]
    unnamed x48 -> x46, local copies, waits for them, and re-layouts: 12.2 us -> 11.9 us
  transfers between devices with their start and end apart: 9 -> 9, of which waited for: 4 -> 4; matrix products, arithmetic and copies ran while one was open for 21% -> 22% of each run, Pallas kernels for 0% -> 0%
where the time goes in v3:
time: 267 us; the launch traced here: 266 us
  waiting for transfers between devices  93.3 us (35%)
  other arithmetic  47.1 us (18%)
  blocking collectives  40.4 us (15%)
  local copies, waits for them, and re-layouts  31.2 us (12%)
  matrix products  25.4 us (10%)
  between operations  15.6 us (6%)
  starting transfers between devices  13.1 us (5%)
    reduce_scatter x3, waiting for transfers between devices, reduce_grads(): part = lax.psum_scatter(part, name, scatter_dimension=0, tiled=True)  68.8 us
    all_gather x2, blocking collectives, reduce_grads(): part = lax.all_gather(part, name, axis=0, tiled=True)  26 us
    reduce_scatter x1, waiting for transfers between devices, reduce_grads(): lax.psum_scatter(part.astype(jnp.bfloat16), 'c', scatter_dimension=0, til...  24.4 us
    unnamed x1, blocking collectives  14.3 us
    unnamed x46, local copies, waits for them, and re-layouts  11.9 us
    scatter-add x1, other arithmetic, slab_backward(): d_extended = d_extended.at[dest + rim].add(d_joined[:, width:2 * width])  10.3 us
    dot_general x4, matrix products, right_dot(): lax.dot_general(first, second, (((1,), (1,)), ((), ())), preferred_elemen...  10.3 us
    scatter-add x1, other arithmetic, slab_backward(): d_extended = d_extended.at[sources].add(d_joined[:, :width])  8.81 us
  transfers between devices with their start and end apart: 9, of which 4 were waited for; matrix products, arithmetic and copies ran while one was open for 22% of the time, Pallas kernels for 0%

profile of v3, /device:TPU:8, one launch (start us, length us, event | category | flops | bytes accessed | tf_op | source)
XLA Modules:
  0.0 266.1 jit_solution(840154584101283073)
XLA Ops:
  7.2 1.1 fusion.38
  8.3 1.3 collective-permute-start.1
  9.6 4.6 %collective-permute-start = (bf16[128,512]{1,0:T(8,128)(2,1)S(1)}, bf16[128,512]{1,0:T(8,128)(2,1)S(1)}, u32[]{:S(2)}, u32[]{:S(2)}) collective-permute-start(bf16[128,512]{1,0:T(8,128)(2,1)S(1)} %get-tuple-element.57), channel_id=1, source_target_pairs={{0,1},{1,2},{2,3},{3,4},{4,5},{5,6},{6,7},{7,8},{8,9},{9,10},{10,1... | collective-permute-start | bytes 393224 | tf_op jit(solution)/shard_map/ppermute | solution.py:16
  14.8 0.7 broadcast_multiply_fusion.3
  15.4 0.8 compare_select_fusion.1
  16.2 1.4 copy.25
  17.8 4.0 %gather_fusion.1 = bf16[1024,512]{1,0:T(8,128)(2,1)S(1)} fusion(bf16[1024,512]{1,0:T(8,128)(2,1)S(1)} %constant_dynamic-update-slice_fusion, s32[1024]{0:T(1024)S(1)} %get-tuple-element.68), kind=kCustom, calls=%fused_computation.1 | custom fusion | bytes 2101248 | tf_op jit(solution)/shard_map/gather | solution.py:78
  21.8 5.1 %gather_fusion = bf16[1024,512]{1,0:T(8,128)(2,1)} fusion(bf16[1024,512]{1,0:T(8,128)(2,1)S(1)} %constant_dynamic-update-slice_fusion, s32[1024]{0:T(1024)S(1)} %get-tuple-element.59), kind=kCustom, calls=%fused_computation | custom fusion | bytes 2101248 | tf_op jit(solution)/shard_map/gather | solution.py:78
  26.8 1.4 constant_dynamic-update-slice_fusion.5
  28.5 1.9 copy-done.9
  30.3 1.8 fusion.11
  32.1 0.8 fusion.39
  32.9 0.6 copy-done.15
  33.5 0.4 multiply_reduce_fusion.1
  33.9 0.5 multiply_convert_fusion.1
  34.6 2.2 fusion.20
  36.8 1.4 broadcast_in_dim.43
  38.2 4.8 %scatter_fusion = f32[6,128,512]{2,1,0:T(8,128)} fusion(f32[6,128,512]{2,1,0:T(8,128)} %broadcast_in_dim.43, s32[8]{0:T(128)S(1)} %get-tuple-element.63, f32[8,128,512]{2,1,0:T(8,128)} %fusion.20), kind=kCustom, calls=%fused_computation.3 | custom fusion | flops 524288 | bytes 6291488 | tf_op jit(solution)/shard_map/scatter-add | solution.py:92
  43.0 1.6 convert_element_type.75
  44.6 2.3 fusion.14
  46.9 0.7 fusion.40
  47.7 0.3 multiply_reduce_fusion.2
  48.1 0.4 fusion.18
  48.5 0.4 add_convert_fusion.1
  48.9 0.6 convolution_convert_fusion.2
  49.5 1.0 multiply_convert_fusion.3
  50.5 2.0 convolution_convert_fusion.1
  52.5 1.0 fusion.15
  53.5 1.7 copy-done
  55.2 1.0 slice.162
  56.2 2.7 %gather_fusion.2 = bf16[8,128,512]{2,1,0:T(8,128)(2,1)} fusion(bf16[6,128,512]{2,1,0:T(8,128)(2,1)} %bitcast.39, s32[1024]{0:T(1024)S(1)} %pad_clamp_fusion), kind=kCustom, calls=%fused_computation.2 | custom fusion | bytes 2097184 | tf_op jit(solution)/shard_map/gather | solution.py:105
  58.9 1.8 fusion.19
  60.7 0.8 multiply_reduce_fusion
  61.6 1.6 fusion.36
  63.2 1.0 convolution_convert_fusion.3
  64.2 2.4 multiply_convert_fusion
  66.6 1.0 copy-done.13
  67.6 1.8 convolution_convert_fusion
  69.5 0.3 pad_maximum_fusion
  69.8 2.0 copy.30
  71.9 24.4 %reduce-scatter.7.cloned.1.call-done = bf16[1792,512]{1,0:T(8,128)(2,1)} async-done(((bf16[3584,512]{1,0:T(8,128)(2,1)}), bf16[1792,512]{1,0:T(8,128)(2,1)}) %reduce-scatter.7.cloned.1.call-update) | async-done | bytes 1835024 | tf_op jit(solution)/shard_map/reduce_scatter | solution.py:137
  96.3 3.8 %convert_element_type.90 = f32[1792,512]{1,0:T(8,128)} convert(bf16[1792,512]{1,0:T(8,128)(2,1)} %reduce-scatter.7.cloned.1.call-done) | non-fusion elementwise | flops 917504 | bytes 5505024 | tf_op jit(solution)/shard_map/convert_element_type | solution.py:138
  100.2 45.3 %reduce-scatter.9.cloned.1.call-done = f32[448,512]{1,0:T(8,128)} async-done(((f32[1792,512]{1,0:T(8,128)}), f32[448,512]{1,0:T(8,128)}) %reduce-scatter.9.cloned.1.call-update) | async-done | bytes 917520 | tf_op jit(solution)/shard_map/reduce_scatter | solution.py:140
  145.6 0.6 dynamic-slice.28
  146.8 1.7 copy.33
  148.5 5.9 %fusion.9 = f32[1024,1536]{1,0:T(8,128)} fusion(bf16[1024,512]{1,0:T(8,128)(2,1)S(1)} %copy-done.14, bf16[3584,512]{1,0:T(8,128)(2,1)} %param.23), kind=kOutput, calls=%fused_computation.38 | convolution fusion | flops 1610612736 | bytes 8912896 | tf_op jit(solution)/shard_map/dot_general | solution.py:57
  154.4 8.8 %scatter_custom_fusion.1 = f32[1024,512]{1,0:T(8,128)} fusion(s32[1024]{0:T(1024)S(1)} %get-tuple-element.58, f32[1024,1536]{1,0:T(8,128)} %fusion.9, f32[]{:T(128)} %constant.111.clone.1), kind=kCustom, calls=%fused_computation.19 | custom fusion | flops 524288 | bytes 4194816 | tf_op jit(solution)/shard_map/scatter-add | solution.py:117
  163.2 10.3 %scatter_custom_fusion.2 = f32[1024,512]{1,0:T(8,128)} fusion(f32[1024,512]{1,0:T(8,128)} %scatter_custom_fusion.1, s32[1024]{0:T(1024)S(1)} %get-tuple-element.69, f32[1024,1536]{1,0:T(8,128)} %fusion.9), kind=kCustom, calls=%fused_computation.17 | custom fusion | flops 524288 | bytes 4194304 | tf_op jit(solution)/shard_map/scatter-add | solution.py:118
  173.5 1.9 copy.27
  175.6 3.5 %collective-permute-start.2 = (bf16[128,512]{0,1:T(8,128)(2,1)S(1)}, bf16[128,512]{0,1:T(8,128)(2,1)S(1)}, u32[]{:S(2)}, u32[]{:S(2)}) collective-permute-start(bf16[128,512]{0,1:T(8,128)(2,1)S(1)} %get-tuple-element.55), channel_id=1, source_target_pairs={{0,1},{1,2},{2,3},{3,4},{4,5},{5,6},{6,7},{7,8},{8,9},{9,10},{10,1... | collective-permute-start | bytes 393224 | tf_op jit(solution)/shard_map/ppermute | solution.py:31
  179.1 8.5 %reduce-scatter.11.cloned.1.call-done = f32[224,512]{1,0:T(8,128)} async-done(((f32[448,512]{1,0:T(8,128)}), f32[224,512]{1,0:T(8,128)}) %reduce-scatter.11.cloned.1.call-update) | async-done | bytes 458768 | tf_op jit(solution)/shard_map/reduce_scatter | solution.py:140
  187.6 2.9 %fusion.8 = f32[768,512]{0,1:T(8,128)} fusion(f32[768,512]{0,1:T(8,128)} %copy.33, bf16[768,512]{0,1:T(8,128)(2,1)S(1)} %copy.25, f32[1024,512]{0,1:T(8,128)S(1)} %copy.27), kind=kLoop, calls=%fused_computation.29 | loop fusion | flops 1179648 | bytes 5505024 | tf_op jit(solution)/shard_map/add | solution.py:119
  190.5 2.9 %fusion.2 = bf16[1024,512]{1,0:T(8,128)(2,1)} fusion(bf16[1024,512]{1,0:T(8,128)(2,1)S(1)} %copy-done.2, f32[1024,1536]{1,0:T(8,128)} %fusion.9), kind=kLoop, calls=%fused_computation.16 | loop fusion | flops 1572864 | bytes 4194304 | tf_op jit(solution)/shard_map/convert_element_type | solution.py:115
  193.4 1.3 collective-permute-start.3
  194.7 1.7 fusion.28
  196.4 15.0 %reduce-scatter.13.cloned.1.call-done = f32[56,512]{1,0:T(8,128)} async-done(((f32[224,512]{1,0:T(8,128)}), f32[56,512]{1,0:T(8,128)}) %reduce-scatter.13.cloned.1.call-update) | async-done | bytes 114704 | tf_op jit(solution)/shard_map/reduce_scatter | solution.py:140
  211.4 14.3 %fusion = f32[16,512]{1,0:T(8,128)S(1)} fusion(f32[56,512]{1,0:T(8,128)} %reduce-scatter.13.cloned.1.call-done), kind=kCustom, calls=%all-reduce-scatter | all-reduce-scatter fusion | flops 32769 | bytes 148480
  225.7 2.4 collective-permute-start.4
  228.1 1.7 fusion.27
  229.9 1.5 convert_element_type.85
  231.4 1.2 copy.31
  232.7 13.4 %all-gather = f32[4,14,512]{2,1,0:T(8,128)S(1)} all-gather(f32[1,14,512]{2,1,0:T(8,128)S(1)} %dynamic-slice_bitcast_fusion), channel_id=1, replica_groups=mesh['zh'=2,'y'=4,'c'=2,'x'=4,'zl'=4] {'zl'}, dimensions={0}, use_global_device_ids=true | all-gather | bytes 143360 | tf_op jit(solution)/shard_map/all_gather | solution.py:142
  246.1 12.7 %all_gather.7 = f32[224,512]{1,0:T(8,128)S(1)} all-gather(f32[56,512]{1,0:T(8,128)S(1)} %reshape.208), channel_id=1, replica_groups=mesh['zh'=2,'y'=4,'c'=2,'x'=4,'zl'=4] {'x'}, dimensions={0}, use_global_device_ids=true | all-gather | bytes 573440 | tf_op jit(solution)/shard_map/all_gather | solution.py:142
  258.7 0.8 broadcast_multiply_fusion
  (65 shorter events, 1.2 us)
Async XLA Ops:
  7.2 10.5 %copy-start.3 = (bf16[768,512]{1,0:T(8,128)(2,1)S(1)}, bf16[768,512]{1,0:T(8,128)(2,1)}, u32[]{:S(2)}) copy-start(bf16[768,512]{1,0:T(8,128)(2,1)} %param.15) | copy-start | bytes 2359300
  7.2 89.1 %reduce-scatter.7.cloned.1.call-start = ((), (), s32[]{:S(2)}) async-start(), calls=%async_computation.4 | async-start | bytes 5505024 | tf_op jit(solution)/shard_map/reduce_scatter | solution.py:137
  8.3 9.5 %collective-permute-start.1 = (bf16[128,512]{1,0:T(8,128)(2,1)S(1)}, bf16[128,512]{1,0:T(8,128)(2,1)S(1)}, u32[]{:S(2)}, u32[]{:S(2)}) collective-permute-start(bf16[128,512]{1,0:T(8,128)(2,1)S(1)} %get-tuple-element.56), channel_id=1, source_target_pairs={{1,0},{2,1},{3,2},{4,3},{5,4},{6,5},{7,6},{8,7},{9,8},{10,9},{11,1... | collective-permute-start | bytes 393224 | tf_op jit(solution)/shard_map/ppermute | solution.py:19
  9.6 8.1 %collective-permute-start = (bf16[128,512]{1,0:T(8,128)(2,1)S(1)}, bf16[128,512]{1,0:T(8,128)(2,1)S(1)}, u32[]{:S(2)}, u32[]{:S(2)}) collective-permute-start(bf16[128,512]{1,0:T(8,128)(2,1)S(1)} %get-tuple-element.57), channel_id=1, source_target_pairs={{0,1},{1,2},{2,3},{3,4},{4,5},{5,6},{6,7},{7,8},{8,9},{9,10},{10,1... | collective-permute-start | bytes 393224 | tf_op jit(solution)/shard_map/ppermute | solution.py:16
  26.8 1.5 copy-start.6
  28.2 2.1 copy-start.9
  30.3 1.8 copy-start.7
  32.1 1.4 copy-start.15
  33.9 0.7 copy-start.11
  43.0 1.6 copy-start.4
  44.6 2.4 copy-start.10
  53.5 1.7 copy-start
  58.9 1.8 copy-start.1
  61.6 1.6 copy-start.16
  64.2 3.4 %copy-start.8 = (bf16[1024,1536]{1,0:T(8,128)(2,1)S(1)}, bf16[1024,1536]{1,0:T(8,128)(2,1)}, u32[]{:S(2)}) copy-start(bf16[1024,1536]{1,0:T(8,128)(2,1)} %copy-done.7) | copy-start | bytes 9437188
  66.6 1.0 copy-start.13
  67.6 1.8 copy-start.5
  71.8 73.7 %reduce-scatter.9.cloned.1.call-start = ((), (), s32[]{:S(2)}) async-start(), calls=%async_computation.5 | async-start | bytes 4587520 | tf_op jit(solution)/shard_map/reduce_scatter | solution.py:140
  100.1 45.4 %copy-start.12 = (u32[256]{0:T(256)S(1)}, u32[256]{0:T(256)}, u32[]{:S(2)}) copy-start(u32[256]{0:T(256)} %constant.126) | copy-start | bytes 3076
  100.1 46.7 %slice-start = ((f32[768,1024]{1,0:T(8,128)}), f32[768,512]{1,0:T(8,128)S(1)}, s32[]{:S(2)}) async-start(f32[768,1024]{1,0:T(8,128)} %copy-done), calls=%async_computation.8 | async-start | bytes 3145728 | tf_op jit(solution)/shard_map/slice | solution.py:120
  100.2 87.4 %reduce-scatter.11.cloned.1.call-start = ((), (), s32[]{:S(2)}) async-start(), calls=%async_computation.6 | async-start | bytes 1376256 | tf_op jit(solution)/shard_map/reduce_scatter | solution.py:140
  145.5 65.9 %reduce-scatter.13.cloned.1.call-start = ((), (), s32[]{:S(2)}) async-start(), calls=%async_computation.7 | async-start | bytes 573440 | tf_op jit(solution)/shard_map/reduce_scatter | solution.py:140
  146.8 1.7 copy-start.14
  175.6 19.0 %collective-permute-start.2 = (bf16[128,512]{0,1:T(8,128)(2,1)S(1)}, bf16[128,512]{0,1:T(8,128)(2,1)S(1)}, u32[]{:S(2)}, u32[]{:S(2)}) collective-permute-start(bf16[128,512]{0,1:T(8,128)(2,1)S(1)} %get-tuple-element.55), channel_id=1, source_target_pairs={{0,1},{1,2},{2,3},{3,4},{4,5},{5,6},{6,7},{7,8},{8,9},{9,10},{10,1... | collective-permute-start | bytes 393224 | tf_op jit(solution)/shard_map/ppermute | solution.py:31
  187.6 2.9 %copy-start.2 = (bf16[1024,512]{1,0:T(8,128)(2,1)S(1)}, bf16[1024,512]{1,0:T(8,128)(2,1)}, u32[]{:S(2)}) copy-start(bf16[1024,512]{1,0:T(8,128)(2,1)} %param.18) | copy-start | bytes 3145732
  193.4 34.8 %collective-permute-start.3 = (bf16[128,512]{0,1:T(8,128)(2,1)S(1)}, bf16[128,512]{0,1:T(8,128)(2,1)S(1)}, u32[]{:S(2)}, u32[]{:S(2)}) collective-permute-start(bf16[128,512]{0,1:T(8,128)(2,1)S(1)} %get-tuple-element.54), channel_id=1, source_target_pairs={{1,0},{2,1},{3,2},{4,3},{5,4},{6,5},{7,6},{8,7},{9,8},{10,9},{11,1... | collective-permute-start | bytes 393224 | tf_op jit(solution)/shard_map/ppermute | solution.py:31
  225.7 6.8 %collective-permute-start.4 = (f32[6,512]{1,0:T(8,128)S(1)}, f32[6,512]{1,0:T(8,128)S(1)}, u32[]{:S(2)}, u32[]{:S(2)}) collective-permute-start(f32[6,512]{1,0:T(8,128)S(1)} %slice.132), channel_id=1, source_target_pairs={{0,1},{1,2},{2,3},{4,5},{5,6},{6,7},{8,9},{9,10},{10,11},{12,13},{... | collective-permute-start | bytes 36872
Sparse Core Ops, SparseCore 0:
  71.9 24.3 reduce-scatter.6
  100.3 45.1 reduce-scatter.8
  148.0 39.5 reduce-scatter.10
  190.0 21.3 reduce-scatter.12

commit v4 on v3

--- a/solution.py
+++ b/solution.py
@@ -138,8 +138,10 @@
     part = part.astype(jnp.float32)
     for name in order[1:] + ("x", "zl"):
         part = lax.psum_scatter(part, name, scatter_dimension=0, tiled=True)
+    part = part.astype(jnp.bfloat16)
     for name in ("zl", "x"):
         part = lax.all_gather(part, name, axis=0, tiled=True)
+    part = part.astype(jnp.float32)
     return part
 
 

time: 267 us -> 266 us (level)
  no operation moved by 1% of the time
where the time goes in v4:
time: 266 us; the launch traced here: 265 us
  waiting for transfers between devices  93.2 us (35%)
  other arithmetic  47.1 us (18%)
  blocking collectives  39.6 us (15%)
  local copies, waits for them, and re-layouts  31.2 us (12%)
  matrix products  25.4 us (10%)
  between operations  15.6 us (6%)
  starting transfers between devices  13.2 us (5%)
    reduce_scatter x3, waiting for transfers between devices, reduce_grads(): part = lax.psum_scatter(part, name, scatter_dimension=0, tiled=True)  68.7 us
    all_gather x2, blocking collectives, reduce_grads(): part = lax.all_gather(part, name, axis=0, tiled=True)  25.3 us
    reduce_scatter x1, waiting for transfers between devices, reduce_grads(): lax.psum_scatter(part.astype(jnp.bfloat16), 'c', scatter_dimension=0, til...  24.4 us
    unnamed x1, blocking collectives  14.3 us
    unnamed x46, local copies, waits for them, and re-layouts  12 us
    scatter-add x1, other arithmetic, slab_backward(): d_extended = d_extended.at[dest + rim].add(d_joined[:, width:2 * width])  10.3 us
    dot_general x4, matrix products, right_dot(): lax.dot_general(first, second, (((1,), (1,)), ((), ())), preferred_elemen...  10.3 us
    scatter-add x1, other arithmetic, slab_backward(): d_extended = d_extended.at[sources].add(d_joined[:, :width])  8.81 us
  transfers between devices with their start and end apart: 9, of which 4 were waited for; matrix products, arithmetic and copies ran while one was open for 22% of the time, Pallas kernels for 0%

profile of v4, /device:TPU:8, one launch (start us, length us, event | category | flops | bytes accessed | tf_op | source)
XLA Modules:
  0.0 265.4 jit_solution(9053621370205360741)
XLA Ops:
  7.2 1.1 fusion.39
  8.3 1.3 collective-permute-start.1
  9.6 4.6 %collective-permute-start = (bf16[128,512]{1,0:T(8,128)(2,1)S(1)}, bf16[128,512]{1,0:T(8,128)(2,1)S(1)}, u32[]{:S(2)}, u32[]{:S(2)}) collective-permute-start(bf16[128,512]{1,0:T(8,128)(2,1)S(1)} %get-tuple-element.57), channel_id=1, source_target_pairs={{0,1},{1,2},{2,3},{3,4},{4,5},{5,6},{6,7},{7,8},{8,9},{9,10},{10,1... | collective-permute-start | bytes 393224 | tf_op jit(solution)/shard_map/ppermute | solution.py:16
  14.8 0.7 broadcast_multiply_fusion.2
  15.4 0.8 compare_select_fusion.1
  16.2 1.4 copy.25
  17.8 4.0 %gather_fusion.1 = bf16[1024,512]{1,0:T(8,128)(2,1)S(1)} fusion(bf16[1024,512]{1,0:T(8,128)(2,1)S(1)} %constant_dynamic-update-slice_fusion, s32[1024]{0:T(1024)S(1)} %get-tuple-element.68), kind=kCustom, calls=%fused_computation.1 | custom fusion | bytes 2101248 | tf_op jit(solution)/shard_map/gather | solution.py:78
  21.8 5.1 %gather_fusion = bf16[1024,512]{1,0:T(8,128)(2,1)} fusion(bf16[1024,512]{1,0:T(8,128)(2,1)S(1)} %constant_dynamic-update-slice_fusion, s32[1024]{0:T(1024)S(1)} %get-tuple-element.59), kind=kCustom, calls=%fused_computation | custom fusion | bytes 2101248 | tf_op jit(solution)/shard_map/gather | solution.py:78
  26.8 1.4 constant_dynamic-update-slice_fusion.5
  28.5 1.9 copy-done.9
  30.3 1.8 fusion.11
  32.1 0.8 fusion.40
  32.9 0.6 copy-done.15
  33.5 0.4 multiply_reduce_fusion.1
  33.9 0.5 multiply_convert_fusion.1
  34.6 2.2 fusion.20
  36.8 1.4 broadcast_in_dim.43
  38.2 4.8 %scatter_fusion = f32[6,128,512]{2,1,0:T(8,128)} fusion(f32[6,128,512]{2,1,0:T(8,128)} %broadcast_in_dim.43, s32[8]{0:T(128)S(1)} %get-tuple-element.63, f32[8,128,512]{2,1,0:T(8,128)} %fusion.20), kind=kCustom, calls=%fused_computation.3 | custom fusion | flops 524288 | bytes 6291488 | tf_op jit(solution)/shard_map/scatter-add | solution.py:92
  43.0 1.6 convert_element_type.81
  44.6 2.3 fusion.14
  46.9 0.7 fusion.41
  47.7 0.3 multiply_reduce_fusion.2
  48.1 0.4 fusion.18
  48.5 0.4 add_convert_fusion.1
  48.9 0.6 convolution_convert_fusion.2
  49.5 0.9 multiply_convert_fusion.3
  50.5 2.0 convolution_convert_fusion.1
  52.5 1.0 fusion.15
  53.5 1.7 copy-done
  55.2 1.0 slice.162
  56.2 2.7 %gather_fusion.2 = bf16[8,128,512]{2,1,0:T(8,128)(2,1)} fusion(bf16[6,128,512]{2,1,0:T(8,128)(2,1)} %bitcast.39, s32[1024]{0:T(1024)S(1)} %pad_clamp_fusion), kind=kCustom, calls=%fused_computation.2 | custom fusion | bytes 2097184 | tf_op jit(solution)/shard_map/gather | solution.py:105
  58.9 1.8 fusion.19
  60.7 0.8 multiply_reduce_fusion
  61.6 1.6 fusion.37
  63.2 1.0 convolution_convert_fusion.3
  64.2 2.4 multiply_convert_fusion
  66.7 1.0 copy-done.13
  67.6 1.8 convolution_convert_fusion
  69.5 0.3 pad_maximum_fusion
  69.8 2.0 copy.30
  71.9 24.4 %reduce-scatter.7.cloned.1.call-done = bf16[1792,512]{1,0:T(8,128)(2,1)} async-done(((bf16[3584,512]{1,0:T(8,128)(2,1)}), bf16[1792,512]{1,0:T(8,128)(2,1)}) %reduce-scatter.7.cloned.1.call-update) | async-done | bytes 1835024 | tf_op jit(solution)/shard_map/reduce_scatter | solution.py:137
  96.3 3.8 %convert_element_type.96 = f32[1792,512]{1,0:T(8,128)} convert(bf16[1792,512]{1,0:T(8,128)(2,1)} %reduce-scatter.7.cloned.1.call-done) | non-fusion elementwise | flops 917504 | bytes 5505024 | tf_op jit(solution)/shard_map/convert_element_type | solution.py:138
  100.2 45.3 %reduce-scatter.9.cloned.1.call-done = f32[448,512]{1,0:T(8,128)} async-done(((f32[1792,512]{1,0:T(8,128)}), f32[448,512]{1,0:T(8,128)}) %reduce-scatter.9.cloned.1.call-update) | async-done | bytes 917520 | tf_op jit(solution)/shard_map/reduce_scatter | solution.py:140
  145.6 0.6 dynamic-slice.28
  146.8 1.7 copy.33
  148.5 5.9 %fusion.9 = f32[1024,1536]{1,0:T(8,128)} fusion(bf16[1024,512]{1,0:T(8,128)(2,1)S(1)} %copy-done.14, bf16[3584,512]{1,0:T(8,128)(2,1)} %param.23), kind=kOutput, calls=%fused_computation.38 | convolution fusion | flops 1610612736 | bytes 8912896 | tf_op jit(solution)/shard_map/dot_general | solution.py:57
  154.4 8.8 %scatter_custom_fusion.1 = f32[1024,512]{1,0:T(8,128)} fusion(s32[1024]{0:T(1024)S(1)} %get-tuple-element.58, f32[1024,1536]{1,0:T(8,128)} %fusion.9, f32[]{:T(128)} %constant.111.clone.1), kind=kCustom, calls=%fused_computation.19 | custom fusion | flops 524288 | bytes 4194816 | tf_op jit(solution)/shard_map/scatter-add | solution.py:117
  163.2 10.3 %scatter_custom_fusion.2 = f32[1024,512]{1,0:T(8,128)} fusion(f32[1024,512]{1,0:T(8,128)} %scatter_custom_fusion.1, s32[1024]{0:T(1024)S(1)} %get-tuple-element.69, f32[1024,1536]{1,0:T(8,128)} %fusion.9), kind=kCustom, calls=%fused_computation.17 | custom fusion | flops 524288 | bytes 4194304 | tf_op jit(solution)/shard_map/scatter-add | solution.py:118
  173.5 1.9 copy.27
  175.6 3.4 %collective-permute-start.2 = (bf16[128,512]{0,1:T(8,128)(2,1)S(1)}, bf16[128,512]{0,1:T(8,128)(2,1)S(1)}, u32[]{:S(2)}, u32[]{:S(2)}) collective-permute-start(bf16[128,512]{0,1:T(8,128)(2,1)S(1)} %get-tuple-element.55), channel_id=1, source_target_pairs={{0,1},{1,2},{2,3},{3,4},{4,5},{5,6},{6,7},{7,8},{8,9},{9,10},{10,1... | collective-permute-start | bytes 393224 | tf_op jit(solution)/shard_map/ppermute | solution.py:31
  179.1 8.5 %reduce-scatter.11.cloned.1.call-done = f32[224,512]{1,0:T(8,128)} async-done(((f32[448,512]{1,0:T(8,128)}), f32[224,512]{1,0:T(8,128)}) %reduce-scatter.11.cloned.1.call-update) | async-done | bytes 458768 | tf_op jit(solution)/shard_map/reduce_scatter | solution.py:140
  187.6 2.9 %fusion.8 = f32[768,512]{0,1:T(8,128)} fusion(f32[768,512]{0,1:T(8,128)} %copy.33, bf16[768,512]{0,1:T(8,128)(2,1)S(1)} %copy.25, f32[1024,512]{0,1:T(8,128)S(1)} %copy.27), kind=kLoop, calls=%fused_computation.29 | loop fusion | flops 1179648 | bytes 5505024 | tf_op jit(solution)/shard_map/add | solution.py:119
  190.5 2.9 %fusion.2 = bf16[1024,512]{1,0:T(8,128)(2,1)} fusion(bf16[1024,512]{1,0:T(8,128)(2,1)S(1)} %copy-done.2, f32[1024,1536]{1,0:T(8,128)} %fusion.9), kind=kLoop, calls=%fused_computation.16 | loop fusion | flops 1572864 | bytes 4194304 | tf_op jit(solution)/shard_map/convert_element_type | solution.py:115
  193.4 1.3 collective-permute-start.3
  194.7 1.7 fusion.28
  196.4 15.0 %reduce-scatter.13.cloned.1.call-done = f32[56,512]{1,0:T(8,128)} async-done(((f32[224,512]{1,0:T(8,128)}), f32[56,512]{1,0:T(8,128)}) %reduce-scatter.13.cloned.1.call-update) | async-done | bytes 114704 | tf_op jit(solution)/shard_map/reduce_scatter | solution.py:140
  211.3 14.3 %fusion = f32[16,512]{1,0:T(8,128)S(1)} fusion(f32[56,512]{1,0:T(8,128)} %reduce-scatter.13.cloned.1.call-done), kind=kCustom, calls=%all-reduce-scatter | all-reduce-scatter fusion | flops 32769 | bytes 148480
  225.7 2.4 collective-permute-start.4
  228.1 1.7 fusion.27
  229.9 1.5 convert_element_type.91
  231.4 1.2 copy.31
  232.7 13.1 %all-gather = bf16[4,14,512]{2,1,0:T(8,128)(2,1)S(1)} all-gather(bf16[1,14,512]{2,1,0:T(8,128)(2,1)S(1)} %fusion.31), channel_id=1, replica_groups=mesh['zh'=2,'y'=4,'c'=2,'x'=4,'zl'=4] {'zl'}, dimensions={0}, use_global_device_ids=true | all-gather | bytes 71680 | tf_op jit(solution)/shard_map/all_gather | solution.py:143
  245.8 12.2 %all_gather.7 = bf16[224,512]{1,0:T(8,128)(2,1)S(1)} all-gather(bf16[56,512]{1,0:T(8,128)(2,1)S(1)} %reshape.208), channel_id=1, replica_groups=mesh['zh'=2,'y'=4,'c'=2,'x'=4,'zl'=4] {'x'}, dimensions={0}, use_global_device_ids=true | all-gather | bytes 286720 | tf_op jit(solution)/shard_map/all_gather | solution.py:143
  258.0 0.8 convert_multiply_fusion.2
  (65 shorter events, 1.2 us)
Async XLA Ops:
  7.2 10.5 %copy-start.3 = (bf16[768,512]{1,0:T(8,128)(2,1)S(1)}, bf16[768,512]{1,0:T(8,128)(2,1)}, u32[]{:S(2)}) copy-start(bf16[768,512]{1,0:T(8,128)(2,1)} %param.15) | copy-start | bytes 2359300
  7.2 89.1 %reduce-scatter.7.cloned.1.call-start = ((), (), s32[]{:S(2)}) async-start(), calls=%async_computation.4 | async-start | bytes 5505024 | tf_op jit(solution)/shard_map/reduce_scatter | solution.py:137
  8.3 9.5 %collective-permute-start.1 = (bf16[128,512]{1,0:T(8,128)(2,1)S(1)}, bf16[128,512]{1,0:T(8,128)(2,1)S(1)}, u32[]{:S(2)}, u32[]{:S(2)}) collective-permute-start(bf16[128,512]{1,0:T(8,128)(2,1)S(1)} %get-tuple-element.56), channel_id=1, source_target_pairs={{1,0},{2,1},{3,2},{4,3},{5,4},{6,5},{7,6},{8,7},{9,8},{10,9},{11,1... | collective-permute-start | bytes 393224 | tf_op jit(solution)/shard_map/ppermute | solution.py:19
  9.6 8.1 %collective-permute-start = (bf16[128,512]{1,0:T(8,128)(2,1)S(1)}, bf16[128,512]{1,0:T(8,128)(2,1)S(1)}, u32[]{:S(2)}, u32[]{:S(2)}) collective-permute-start(bf16[128,512]{1,0:T(8,128)(2,1)S(1)} %get-tuple-element.57), channel_id=1, source_target_pairs={{0,1},{1,2},{2,3},{3,4},{4,5},{5,6},{6,7},{7,8},{8,9},{9,10},{10,1... | collective-permute-start | bytes 393224 | tf_op jit(solution)/shard_map/ppermute | solution.py:16
  26.8 1.5 copy-start.6
  28.2 2.1 copy-start.9
  30.3 1.8 copy-start.7
  32.1 1.4 copy-start.15
  33.9 0.7 copy-start.11
  43.0 1.6 copy-start.4
  44.6 2.4 copy-start.10
  53.5 1.7 copy-start
  58.9 1.8 copy-start.1
  61.6 1.6 copy-start.16
  64.2 3.4 %copy-start.8 = (bf16[1024,1536]{1,0:T(8,128)(2,1)S(1)}, bf16[1024,1536]{1,0:T(8,128)(2,1)}, u32[]{:S(2)}) copy-start(bf16[1024,1536]{1,0:T(8,128)(2,1)} %copy-done.7) | copy-start | bytes 9437188
  66.6 1.0 copy-start.13
  67.6 1.8 copy-start.5
  71.8 73.6 %reduce-scatter.9.cloned.1.call-start = ((), (), s32[]{:S(2)}) async-start(), calls=%async_computation.5 | async-start | bytes 4587520 | tf_op jit(solution)/shard_map/reduce_scatter | solution.py:140
  100.1 45.4 %copy-start.12 = (u32[256]{0:T(256)S(1)}, u32[256]{0:T(256)}, u32[]{:S(2)}) copy-start(u32[256]{0:T(256)} %constant.126) | copy-start | bytes 3076
  100.2 46.6 %slice-start = ((f32[768,1024]{1,0:T(8,128)}), f32[768,512]{1,0:T(8,128)S(1)}, s32[]{:S(2)}) async-start(f32[768,1024]{1,0:T(8,128)} %copy-done), calls=%async_computation.8 | async-start | bytes 3145728 | tf_op jit(solution)/shard_map/slice | solution.py:120
  100.2 87.4 %reduce-scatter.11.cloned.1.call-start = ((), (), s32[]{:S(2)}) async-start(), calls=%async_computation.6 | async-start | bytes 1376256 | tf_op jit(solution)/shard_map/reduce_scatter | solution.py:140
  145.5 65.9 %reduce-scatter.13.cloned.1.call-start = ((), (), s32[]{:S(2)}) async-start(), calls=%async_computation.7 | async-start | bytes 573440 | tf_op jit(solution)/shard_map/reduce_scatter | solution.py:140
  146.8 1.7 copy-start.14
  175.6 19.0 %collective-permute-start.2 = (bf16[128,512]{0,1:T(8,128)(2,1)S(1)}, bf16[128,512]{0,1:T(8,128)(2,1)S(1)}, u32[]{:S(2)}, u32[]{:S(2)}) collective-permute-start(bf16[128,512]{0,1:T(8,128)(2,1)S(1)} %get-tuple-element.55), channel_id=1, source_target_pairs={{0,1},{1,2},{2,3},{3,4},{4,5},{5,6},{6,7},{7,8},{8,9},{9,10},{10,1... | collective-permute-start | bytes 393224 | tf_op jit(solution)/shard_map/ppermute | solution.py:31
  187.6 2.9 %copy-start.2 = (bf16[1024,512]{1,0:T(8,128)(2,1)S(1)}, bf16[1024,512]{1,0:T(8,128)(2,1)}, u32[]{:S(2)}) copy-start(bf16[1024,512]{1,0:T(8,128)(2,1)} %param.18) | copy-start | bytes 3145732
  193.4 34.8 %collective-permute-start.3 = (bf16[128,512]{0,1:T(8,128)(2,1)S(1)}, bf16[128,512]{0,1:T(8,128)(2,1)S(1)}, u32[]{:S(2)}, u32[]{:S(2)}) collective-permute-start(bf16[128,512]{0,1:T(8,128)(2,1)S(1)} %get-tuple-element.54), channel_id=1, source_target_pairs={{1,0},{2,1},{3,2},{4,3},{5,4},{6,5},{7,6},{8,7},{9,8},{10,9},{11,1... | collective-permute-start | bytes 393224 | tf_op jit(solution)/shard_map/ppermute | solution.py:31
  225.7 6.8 %collective-permute-start.4 = (bf16[6,512]{1,0:T(8,128)(2,1)S(1)}, bf16[6,512]{1,0:T(8,128)(2,1)S(1)}, u32[]{:S(2)}, u32[]{:S(2)}) collective-permute-start(bf16[6,512]{1,0:T(8,128)(2,1)S(1)} %slice.132), channel_id=1, source_target_pairs={{0,1},{1,2},{2,3},{4,5},{5,6},{6,7},{8,9},{9,10},{10,11},{12,13},{... | collective-permute-start | bytes 18440
Sparse Core Ops, SparseCore 0:
  71.9 24.3 reduce-scatter.6
  100.3 45.1 reduce-scatter.8
  148.0 39.5 reduce-scatter.10
  190.0 21.3 reduce-scatter.12
